TPU v7x, 32 devices: a whole 2x2x4 slice. The times are simulated.
32 devices in a mesh: gx: 4 (over z), gy: 4 (over y, core), gz: 2 (over x).
Axes of the slice: x: 2, y: 2, z: 4, core: 2. Of those that a mesh axis runs over, the one named last changes fastest.
Arguments:
- solution: float32 [64, 64, 256], P('gx', 'gy', 'gz'), may hold values from -6 to 6
- right_side: float32 [64, 64, 256], P('gx', 'gy', 'gz'), may hold values from -6 to 6
Outputs:
- improved: float32 [64, 64, 256], P('gx', 'gy', 'gz')
All inputs are finite; a program needn't handle non-finite values.
Results may differ from a plain program's by a relative error of at most 0.00015.
Values sent between devices are 32-bit elements; how exact they have to be, the bound alone decides.
A program may use at most 64 MiB of HBM per device.

v0:
```python
import jax
import jax.numpy as jnp
from jax import lax
from jax.sharding import PartitionSpec as P

LEVELS = 3
SWEEPS = 2


stiff_matrix = (
    (7.0 / 3.0, -8.0 / 3.0, 1.0 / 3.0),
    (-8.0 / 3.0, 16.0 / 3.0, -8.0 / 3.0),
    (1.0 / 3.0, -8.0 / 3.0, 7.0 / 3.0),
)
mass_matrix = (
    (4.0 / 30.0, 2.0 / 30.0, -1.0 / 30.0),
    (2.0 / 30.0, 16.0 / 30.0, 2.0 / 30.0),
    (-1.0 / 30.0, 2.0 / 30.0, 4.0 / 30.0),
)
cheb_centre = 1.32
cheb_half = 1.1
cheb_sigma = 1.2


def extended_2(value, sides, width):
    for axis, dim in sides:
        count, length = (lax.axis_size(axis), value.shape[dim])
        up = [(i, (i + 1) % count) for i in range(count - 1)]
        down = [(j, i) for i, j in up]
        last = lax.slice_in_dim(value, length - width, length, axis=dim)
        leading = lax.slice_in_dim(value, 0, width, axis=dim)
        before = lax.ppermute(last, axis, up)
        after = lax.ppermute(leading, axis, down)
        value = jnp.concatenate([before, value, after], axis=dim)
    return value


def from_behind(value, axis, by):
    count = lax.axis_size(axis)
    pairs = [(i, i + by) for i in range(count) if 0 <= i + by < count]
    return lax.ppermute(value, axis, pairs)


def along_axis(values, dim_index, matrix):
    inner_len = values.shape[dim_index] - 4
    parity = jnp.arange(inner_len) % 2 == 0
    vertex = (matrix[2][0], matrix[2][1], matrix[2][2] + matrix[0][0], matrix[0][1], matrix[0][2])
    middle = (0.0, matrix[1][0], matrix[1][1], matrix[1][2], 0.0)
    shape_list = [1, 1, 1]
    shape_list[dim_index] = inner_len
    summed = None
    for offset in range(5):
        weight = (
            jnp.where(parity, vertex[offset], middle[offset])
            .astype(jnp.float32)
            .reshape(shape_list)
        )
        shifted = lax.slice_in_dim(values, offset, offset + inner_len, 1, dim_index)
        summed = weight * shifted if offset == 0 else summed + weight * shifted
    return summed


def apply_operator(padded, level_num):
    mass_z = along_axis(padded, 2, mass_matrix)
    stiff_z = along_axis(padded, 2, stiff_matrix)
    mass_yz = along_axis(mass_z, 1, mass_matrix)
    stiff_y = along_axis(mass_z, 1, stiff_matrix)
    stiff_only_z = along_axis(stiff_z, 1, mass_matrix)
    return 2.0**level_num * (
        along_axis(mass_yz, 0, stiff_matrix) + along_axis(stiff_y + stiff_only_z, 0, mass_matrix)
    )


def inverse_diagonal(new_shape, level_num):
    stiff_list = []
    mass_list = []
    for dim_index in range(3):
        even_node = jnp.arange(new_shape[dim_index]) % 2 == 0
        shape_list = [1, 1, 1]
        shape_list[dim_index] = new_shape[dim_index]
        stiff_list.append(
            jnp.where(even_node, 14.0 / 3.0, 16.0 / 3.0).astype(jnp.float32).reshape(shape_list)
        )
        mass_list.append(
            jnp.where(even_node, 8.0 / 30.0, 16.0 / 30.0).astype(jnp.float32).reshape(shape_list)
        )
    stiff_first, stiff_second, stiff_third = stiff_list
    mass_first, mass_second, mass_third = mass_list
    diagonal = 2.0**level_num * (
        stiff_first * mass_second * mass_third
        + mass_first * stiff_second * mass_third
        + mass_first * mass_second * stiff_third
    )
    return 1.0 / diagonal


def along_dim_product(matrix, values, dim_index):
    einsum_forms = ("ap,pyz->ayz", "ap,xpz->xaz", "ap,xyp->xya")
    return jnp.einsum(einsum_forms[dim_index], matrix, values, precision=lax.Precision.HIGHEST)


def prolong_matrix(fine_count, coarse_len):
    row_index = jnp.arange(fine_count + 4)[:, None]
    col_index = jnp.arange(coarse_len)[None, :]
    half_index = row_index // 2
    offset = col_index - half_index
    even_row = row_index % 2 == 0
    even_half = half_index % 2 == 0
    odd_even = jnp.where(
        offset == 0, -0.125, jnp.where(offset == 1, 0.75, jnp.where(offset == 2, 0.375, 0.0))
    )
    odd_odd = jnp.where(
        offset == 1, 0.375, jnp.where(offset == 2, 0.75, jnp.where(offset == 3, -0.125, 0.0))
    )
    vertex = jnp.where(offset == 1, 1.0, 0.0)
    entries = jnp.where(even_row, vertex, jnp.where(even_half, odd_even, odd_odd))
    entries = jnp.where(row_index == fine_count + 3, 0.0, entries)
    return entries.astype(jnp.float32)


def restrict_matrix(coarse_count, length):
    row_index = jnp.arange(coarse_count)[:, None]
    col_index = jnp.arange(length)[None, :]
    offset = col_index - 2 * row_index
    even_row = row_index % 2 == 0
    outer = jnp.where(even_row, -0.125, 0.0)
    inner = jnp.where(even_row, 0.375, 0.75)
    entries = jnp.where(
        offset == 3,
        1.0,
        jnp.where(
            (offset == 0) | (offset == 6),
            outer,
            jnp.where((offset == 2) | (offset == 4), inner, 0.0),
        ),
    )
    return entries.astype(jnp.float32)


def prolongate(values, fine_shape):
    for dim_index in range(3):
        matrix = prolong_matrix(fine_shape[dim_index], values.shape[dim_index])
        values = along_dim_product(matrix, values, dim_index)
    return values


def restrict_residual(values, coarse_shape):
    for dim_index in range(3):
        matrix = restrict_matrix(coarse_shape[dim_index], values.shape[dim_index])
        values = along_dim_product(matrix, values, dim_index)
    return values


def trim_rim(values, rim_width):
    if rim_width == 0:
        return values
    return values[rim_width:-rim_width, rim_width:-rim_width, rim_width:-rim_width]


def inside_range(extent, rim_width, device_index, device_count):
    owned_len = extent - 2 * rim_width
    position = device_index * owned_len - rim_width + jnp.arange(extent)
    return (position >= 0) & (position < owned_len * device_count)


def interior_mask(new_shape, rim_width):
    first = inside_range(new_shape[0], rim_width, lax.axis_index("gx"), lax.axis_size("gx"))
    second = inside_range(new_shape[1], rim_width, lax.axis_index("gy"), lax.axis_size("gy"))
    third = inside_range(new_shape[2], rim_width, lax.axis_index("gz"), lax.axis_size("gz"))
    return first[:, None, None] & second[None, :, None] & third[None, None, :]


def node_halo(values):
    return extended_2(values, (("gx", 0), ("gy", 1), ("gz", 2)), 2)


def lower_rim(values):
    below = from_behind(values[-3:, :, :], "gx", 1)
    values = jnp.concatenate([below, values], axis=0)
    below = from_behind(values[:, -3:, :], "gy", 1)
    values = jnp.concatenate([below, values], axis=1)
    below = from_behind(values[:, :, -3:], "gz", 1)
    return jnp.concatenate([below, values], axis=2)


def chebyshev(level_num, solution, residual):
    inverse = inverse_diagonal(residual.shape, level_num)
    direction = inverse * residual * (1.0 / cheb_centre)
    solution = solution + direction
    ratio = 1.0 / cheb_sigma
    residual = residual - apply_operator(node_halo(direction), level_num)
    ratio_next = 1.0 / (2.0 * cheb_sigma - ratio)
    direction = ratio_next * ratio * direction + 2.0 * ratio_next / cheb_half * (inverse * residual)
    solution = solution + direction
    return (solution, residual, direction)


def coarse_block_solve(level_num, residual):
    rim_width = 2 * SWEEPS
    padded = extended_2(residual, (("gx", 0), ("gy", 1), ("gz", 2)), rim_width)
    inverse = inverse_diagonal(padded.shape, level_num)
    direction = inverse * padded * (1.0 / cheb_centre)
    solution = trim_rim(direction, rim_width - 2)
    ratio = 1.0 / cheb_sigma
    rim_width = rim_width - 2
    padded = trim_rim(padded, 2) - apply_operator(direction, level_num)
    padded = jnp.where(interior_mask(padded.shape, rim_width), padded, 0.0)
    inverse = trim_rim(inverse, 2)
    ratio_next = 1.0 / (2.0 * cheb_sigma - ratio)
    direction = ratio_next * ratio * trim_rim(direction, 2) + 2.0 * ratio_next / cheb_half * (
        inverse * padded
    )
    solution = solution + trim_rim(direction, rim_width - 2)
    return solution


def vcycle(level_num, solution, residual):
    last_level = level_num == LEVELS - 1
    if last_level:
        return coarse_block_solve(level_num, residual)
    solution, residual, direction = chebyshev(level_num, solution, residual)
    coarse_shape = tuple((extent // 2 for extent in residual.shape))
    residual = residual - apply_operator(node_halo(direction), level_num)
    rim_residual = lower_rim(residual)
    coarse_rhs = restrict_residual(rim_residual, coarse_shape)
    coarse_ext = vcycle(level_num + 1, jnp.zeros_like(coarse_rhs), coarse_rhs)
    extended = prolongate(coarse_ext, residual.shape)
    extended = jnp.where(interior_mask(extended.shape, 2), extended, 0.0)
    solution = solution + trim_rim(extended, 2)
    residual = residual - apply_operator(extended, level_num)
    solution, residual, direction = chebyshev(level_num, solution, residual)
    if level_num == 0:
        return solution
    return node_halo(solution)


def local(solution, right_side):
    residual = right_side - apply_operator(node_halo(solution), 0)
    return vcycle(0, solution, residual)


def solution(mesh):
    placed = (P("gx", "gy", "gz"), P("gx", "gy", "gz"))
    return jax.shard_map(
        local, mesh=mesh, in_specs=placed, out_specs=P("gx", "gy", "gz"), check_vma=False
    )
```

profile of v0, /device:TPU:1, one launch (start us, length us, event | category | flops | bytes accessed | tf_op | source)
XLA Modules:
  0.0 274.4 jit_solution(9566030759017847342)
XLA Ops:
  2.1 4.6 %collective-permute-start = (f32[2,16,128]{2,1,0:T(8,128)S(1)}, f32[2,16,128]{2,1,0:T(8,128)S(1)}, u32[]{:S(2)}, u32[]{:S(2)}) collective-permute-start(f32[2,16,128]{2,1,0:T(8,128)S(1)} %get-tuple-element.62), channel_id=1, source_target_pairs={{0,8},{8,16},{16,24},{1,9},{9,17},{17,25},{2,10},{10,18},{18,26},{... | collective-permute-start | bytes 49160 | tf_op jit(solution)/shard_map/ppermute | solution.py:32
  7.7 5.0 %collective-permute-start.2 = (f32[20,2,128]{2,1,0:T(2,128)S(1)}, f32[20,2,128]{2,1,0:T(2,128)S(1)}, u32[]{:S(2)}, u32[]{:S(2)}) collective-permute-start(f32[20,2,128]{2,1,0:T(2,128)S(1)} %get-tuple-element.53), channel_id=1, source_target_pairs={{0,2},{2,4},{4,6},{1,3},{3,5},{5,7},{8,10},{10,12},{12,14},{9,11},... | collective-permute-start | bytes 61448 | tf_op jit(solution)/shard_map/ppermute | solution.py:32
  12.7 1.9 collective-permute-start.3
  14.6 3.2 %collective-permute-done.3 = f32[20,2,128]{2,1,0:T(2,128)S(1)} collective-permute-done((f32[20,2,128]{2,1,0:T(2,128)S(1)}, f32[20,2,128]{2,1,0:T(2,128)S(1)}, u32[]{:S(2)}, u32[]{:S(2)}) %collective-permute-start.3) | collective-permute-done | bytes 20512 | tf_op jit(solution)/shard_map/ppermute | solution.py:33
  17.9 3.1 %collective-permute-start.4 = (f32[20,20,2]{2,1,0:T(8,128)S(1)}, f32[20,20,2]{2,1,0:T(8,128)S(1)}, u32[]{:S(2)}, u32[]{:S(2)}) collective-permute-start(f32[20,20,2]{2,1,0:T(8,128)S(1)} %get-tuple-element.37), channel_id=1, source_target_pairs={{0,1},{2,3},{4,5},{6,7},{8,9},{10,11},{12,13},{14,15},{16,17},{18,... | collective-permute-start | bytes 9608 | tf_op jit(solution)/shard_map/ppermute | solution.py:32
  22.4 2.9 %collective-permute-done.4 = f32[20,20,2]{2,1,0:T(8,128)S(1)} collective-permute-done((f32[20,20,2]{2,1,0:T(8,128)S(1)}, f32[20,20,2]{2,1,0:T(8,128)S(1)}, u32[]{:S(2)}, u32[]{:S(2)}) %collective-permute-start.4) | collective-permute-done | bytes 3232 | tf_op jit(solution)/shard_map/ppermute | solution.py:32
  25.3 4.1 %collective-permute-done.5 = f32[20,20,2]{2,1,0:T(8,128)S(1)} collective-permute-done((f32[20,20,2]{2,1,0:T(8,128)S(1)}, f32[20,20,2]{2,1,0:T(8,128)S(1)}, u32[]{:S(2)}, u32[]{:S(2)}) %collective-permute-start.5) | collective-permute-done | bytes 3232 | tf_op jit(solution)/shard_map/ppermute | solution.py:33
  31.1 3.9 %collective-permute-start.6 = (f32[2,16,128]{2,1,0:T(8,128)S(1)}, f32[2,16,128]{2,1,0:T(8,128)S(1)}, u32[]{:S(2)}, u32[]{:S(2)}) collective-permute-start(f32[2,16,128]{2,1,0:T(8,128)S(1)} %get-tuple-element.59), channel_id=1, source_target_pairs={{0,8},{8,16},{16,24},{1,9},{9,17},{17,25},{2,10},{10,18},{18,26},{... | collective-permute-start | bytes 49160 | tf_op jit(solution)/shard_map/ppermute | solution.py:32
  36.3 3.5 %collective-permute-done.7 = f32[2,16,128]{2,1,0:T(8,128)S(1)} collective-permute-done((f32[2,16,128]{2,1,0:T(8,128)S(1)}, f32[2,16,128]{2,1,0:T(8,128)S(1)}, u32[]{:S(2)}, u32[]{:S(2)}) %collective-permute-start.7) | collective-permute-done | bytes 16416 | tf_op jit(solution)/shard_map/ppermute | solution.py:33
  39.8 3.1 %collective-permute-start.8 = (f32[20,2,128]{2,1,0:T(2,128)S(1)}, f32[20,2,128]{2,1,0:T(2,128)S(1)}, u32[]{:S(2)}, u32[]{:S(2)}) collective-permute-start(f32[20,2,128]{2,1,0:T(2,128)S(1)} %get-tuple-element.51), channel_id=1, source_target_pairs={{0,2},{2,4},{4,6},{1,3},{3,5},{5,7},{8,10},{10,12},{12,14},{9,11},... | collective-permute-start | bytes 61448 | tf_op jit(solution)/shard_map/ppermute | solution.py:32
  42.9 1.9 collective-permute-start.9
  44.9 3.2 %collective-permute-done.9 = f32[20,2,128]{2,1,0:T(2,128)S(1)} collective-permute-done((f32[20,2,128]{2,1,0:T(2,128)S(1)}, f32[20,2,128]{2,1,0:T(2,128)S(1)}, u32[]{:S(2)}, u32[]{:S(2)}) %collective-permute-start.9) | collective-permute-done | bytes 20512 | tf_op jit(solution)/shard_map/ppermute | solution.py:33
  50.8 2.8 %collective-permute-done.10 = f32[20,20,2]{2,1,0:T(8,128)S(1)} collective-permute-done((f32[20,20,2]{2,1,0:T(8,128)S(1)}, f32[20,20,2]{2,1,0:T(8,128)S(1)}, u32[]{:S(2)}, u32[]{:S(2)}) %collective-permute-start.10) | collective-permute-done | bytes 3232 | tf_op jit(solution)/shard_map/ppermute | solution.py:32
  53.6 4.1 %collective-permute-done.11 = f32[20,20,2]{2,1,0:T(8,128)S(1)} collective-permute-done((f32[20,20,2]{2,1,0:T(8,128)S(1)}, f32[20,20,2]{2,1,0:T(8,128)S(1)}, u32[]{:S(2)}, u32[]{:S(2)}) %collective-permute-start.11) | collective-permute-done | bytes 3232 | tf_op jit(solution)/shard_map/ppermute | solution.py:33
  59.0 3.2 %collective-permute-start.12 = (f32[2,16,128]{2,1,0:T(8,128)S(1)}, f32[2,16,128]{2,1,0:T(8,128)S(1)}, u32[]{:S(2)}, u32[]{:S(2)}) collective-permute-start(f32[2,16,128]{2,1,0:T(8,128)S(1)} %get-tuple-element.57), channel_id=1, source_target_pairs={{0,8},{8,16},{16,24},{1,9},{9,17},{17,25},{2,10},{10,18},{18,26},{... | collective-permute-start | bytes 49160 | tf_op jit(solution)/shard_map/ppermute | solution.py:32
  63.6 3.6 %collective-permute-done.13 = f32[2,16,128]{2,1,0:T(8,128)S(1)} collective-permute-done((f32[2,16,128]{2,1,0:T(8,128)S(1)}, f32[2,16,128]{2,1,0:T(8,128)S(1)}, u32[]{:S(2)}, u32[]{:S(2)}) %collective-permute-start.13) | collective-permute-done | bytes 16416 | tf_op jit(solution)/shard_map/ppermute | solution.py:33
  67.2 3.0 %collective-permute-start.14 = (f32[20,2,128]{2,1,0:T(2,128)S(1)}, f32[20,2,128]{2,1,0:T(2,128)S(1)}, u32[]{:S(2)}, u32[]{:S(2)}) collective-permute-start(f32[20,2,128]{2,1,0:T(2,128)S(1)} %get-tuple-element.49), channel_id=1, source_target_pairs={{0,2},{2,4},{4,6},{1,3},{3,5},{5,7},{8,10},{10,12},{12,14},{9,11},... | collective-permute-start | bytes 61448 | tf_op jit(solution)/shard_map/ppermute | solution.py:32
  70.2 1.9 collective-permute-start.15
  72.1 3.2 %collective-permute-done.15 = f32[20,2,128]{2,1,0:T(2,128)S(1)} collective-permute-done((f32[20,2,128]{2,1,0:T(2,128)S(1)}, f32[20,2,128]{2,1,0:T(2,128)S(1)}, u32[]{:S(2)}, u32[]{:S(2)}) %collective-permute-start.15) | collective-permute-done | bytes 20512 | tf_op jit(solution)/shard_map/ppermute | solution.py:33
  78.1 2.8 %collective-permute-done.16 = f32[20,20,2]{2,1,0:T(8,128)S(1)} collective-permute-done((f32[20,20,2]{2,1,0:T(8,128)S(1)}, f32[20,20,2]{2,1,0:T(8,128)S(1)}, u32[]{:S(2)}, u32[]{:S(2)}) %collective-permute-start.16) | collective-permute-done | bytes 3232 | tf_op jit(solution)/shard_map/ppermute | solution.py:32
  80.9 4.1 %collective-permute-done.17 = f32[20,20,2]{2,1,0:T(8,128)S(1)} collective-permute-done((f32[20,20,2]{2,1,0:T(8,128)S(1)}, f32[20,20,2]{2,1,0:T(8,128)S(1)}, u32[]{:S(2)}, u32[]{:S(2)}) %collective-permute-start.17) | collective-permute-done | bytes 3232 | tf_op jit(solution)/shard_map/ppermute | solution.py:33
  86.2 3.2 %collective-permute-start.18 = (f32[3,16,128]{2,1,0:T(8,128)S(1)}, f32[3,16,128]{2,1,0:T(8,128)S(1)}, u32[]{:S(2)}, u32[]{:S(2)}) collective-permute-start(f32[3,16,128]{2,1,0:T(8,128)S(1)} %slice.1422), channel_id=1, source_target_pairs={{0,8},{8,16},{16,24},{1,9},{9,17},{17,25},{2,10},{10,18},{18,26},{... | collective-permute-start | bytes 73736 | tf_op jit(solution)/shard_map/ppermute | solution.py:41
  90.4 2.8 %collective-permute-start.19 = (f32[19,3,128]{2,1,0:T(4,128)S(1)}, f32[19,3,128]{2,1,0:T(4,128)S(1)}, u32[]{:S(2)}, u32[]{:S(2)}) collective-permute-start(f32[19,3,128]{2,1,0:T(4,128)S(1)} %pad_maximum_fusion.22), channel_id=1, source_target_pairs={{0,2},{2,4},{4,6},{1,3},{3,5},{5,7},{8,10},{10,12},{12,14},{9,11},... | collective-permute-start | bytes 87560 | tf_op jit(solution)/shard_map/ppermute | solution.py:41
  95.8 5.5 %collective-permute-done.20 = f32[19,19,3]{2,1,0:T(8,128)S(1)} collective-permute-done((f32[19,19,3]{2,1,0:T(8,128)S(1)}, f32[19,19,3]{2,1,0:T(8,128)S(1)}, u32[]{:S(2)}, u32[]{:S(2)}) %collective-permute-start.20) | collective-permute-done | bytes 4364 | tf_op jit(solution)/shard_map/ppermute | solution.py:41
  102.5 3.6 %collective-permute-start.21 = (f32[2,8,64]{2,1,0:T(8,128)S(1)}, f32[2,8,64]{2,1,0:T(8,128)S(1)}, u32[]{:S(2)}, u32[]{:S(2)}) collective-permute-start(f32[2,8,64]{2,1,0:T(8,128)S(1)} %get-tuple-element.107), channel_id=1, source_target_pairs={{0,8},{8,16},{16,24},{1,9},{9,17},{17,25},{2,10},{10,18},{18,26},{... | collective-permute-start | bytes 12296 | tf_op jit(solution)/shard_map/ppermute | solution.py:32
  107.5 3.1 %collective-permute-done.22 = f32[2,8,64]{2,1,0:T(8,128)S(1)} collective-permute-done((f32[2,8,64]{2,1,0:T(8,128)S(1)}, f32[2,8,64]{2,1,0:T(8,128)S(1)}, u32[]{:S(2)}, u32[]{:S(2)}) %collective-permute-start.22) | collective-permute-done | bytes 4128 | tf_op jit(solution)/shard_map/ppermute | solution.py:33
  110.6 4.2 %collective-permute-start.23 = (f32[12,2,64]{2,1,0:T(2,128)S(1)}, f32[12,2,64]{2,1,0:T(2,128)S(1)}, u32[]{:S(2)}, u32[]{:S(2)}) collective-permute-start(f32[12,2,64]{2,1,0:T(2,128)S(1)} %get-tuple-element.99), channel_id=1, source_target_pairs={{0,2},{2,4},{4,6},{1,3},{3,5},{5,7},{8,10},{10,12},{12,14},{9,11},... | collective-permute-start | bytes 18440 | tf_op jit(solution)/shard_map/ppermute | solution.py:32
  114.8 1.9 collective-permute-start.24
  116.7 3.1 %collective-permute-done.24 = f32[12,2,64]{2,1,0:T(2,128)S(1)} collective-permute-done((f32[12,2,64]{2,1,0:T(2,128)S(1)}, f32[12,2,64]{2,1,0:T(2,128)S(1)}, u32[]{:S(2)}, u32[]{:S(2)}) %collective-permute-start.24) | collective-permute-done | bytes 6176 | tf_op jit(solution)/shard_map/ppermute | solution.py:33
  119.9 4.1 %collective-permute-start.25 = (f32[12,12,2]{2,1,0:T(8,128)S(1)}, f32[12,12,2]{2,1,0:T(8,128)S(1)}, u32[]{:S(2)}, u32[]{:S(2)}) collective-permute-start(f32[12,12,2]{2,1,0:T(8,128)S(1)} %get-tuple-element.85), channel_id=1, source_target_pairs={{0,1},{2,3},{4,5},{6,7},{8,9},{10,11},{12,13},{14,15},{16,17},{18,... | collective-permute-start | bytes 3464 | tf_op jit(solution)/shard_map/ppermute | solution.py:32
  125.7 3.7 %collective-permute-done.26 = f32[12,12,2]{2,1,0:T(8,128)S(1)} collective-permute-done((f32[12,12,2]{2,1,0:T(8,128)S(1)}, f32[12,12,2]{2,1,0:T(8,128)S(1)}, u32[]{:S(2)}, u32[]{:S(2)}) %collective-permute-start.26) | collective-permute-done | bytes 1184 | tf_op jit(solution)/shard_map/ppermute | solution.py:33
  130.1 1.6 collective-permute-start.27
  133.1 3.1 %collective-permute-done.28 = f32[2,8,64]{2,1,0:T(8,128)S(1)} collective-permute-done((f32[2,8,64]{2,1,0:T(8,128)S(1)}, f32[2,8,64]{2,1,0:T(8,128)S(1)}, u32[]{:S(2)}, u32[]{:S(2)}) %collective-permute-start.28) | collective-permute-done | bytes 4128 | tf_op jit(solution)/shard_map/ppermute | solution.py:33
  136.2 4.8 %collective-permute-start.29 = (f32[12,2,64]{2,1,0:T(2,128)S(1)}, f32[12,2,64]{2,1,0:T(2,128)S(1)}, u32[]{:S(2)}, u32[]{:S(2)}) collective-permute-start(f32[12,2,64]{2,1,0:T(2,128)S(1)} %get-tuple-element.97), channel_id=1, source_target_pairs={{0,2},{2,4},{4,6},{1,3},{3,5},{5,7},{8,10},{10,12},{12,14},{9,11},... | collective-permute-start | bytes 18440 | tf_op jit(solution)/shard_map/ppermute | solution.py:32
  141.0 1.9 collective-permute-start.30
  143.0 3.1 %collective-permute-done.30 = f32[12,2,64]{2,1,0:T(2,128)S(1)} collective-permute-done((f32[12,2,64]{2,1,0:T(2,128)S(1)}, f32[12,2,64]{2,1,0:T(2,128)S(1)}, u32[]{:S(2)}, u32[]{:S(2)}) %collective-permute-start.30) | collective-permute-done | bytes 6176 | tf_op jit(solution)/shard_map/ppermute | solution.py:33
  149.1 3.7 %collective-permute-done.32 = f32[12,12,2]{2,1,0:T(8,128)S(1)} collective-permute-done((f32[12,12,2]{2,1,0:T(8,128)S(1)}, f32[12,12,2]{2,1,0:T(8,128)S(1)}, u32[]{:S(2)}, u32[]{:S(2)}) %collective-permute-start.32) | collective-permute-done | bytes 1184 | tf_op jit(solution)/shard_map/ppermute | solution.py:33
  153.5 1.6 collective-permute-start.33
  156.0 4.2 %collective-permute-start.34 = (f32[11,3,64]{2,1,0:T(4,128)S(1)}, f32[11,3,64]{2,1,0:T(4,128)S(1)}, u32[]{:S(2)}, u32[]{:S(2)}) collective-permute-start(f32[11,3,64]{2,1,0:T(4,128)S(1)} %pad_maximum_fusion.24), channel_id=1, source_target_pairs={{0,2},{2,4},{4,6},{1,3},{3,5},{5,7},{8,10},{10,12},{12,14},{9,11},... | collective-permute-start | bytes 25352 | tf_op jit(solution)/shard_map/ppermute | solution.py:41
  162.5 1.5 collective-permute-done.35
  166.1 4.5 %collective-permute-start.36 = (f32[4,4,32]{2,1,0:T(4,128)S(1)}, f32[4,4,32]{2,1,0:T(4,128)S(1)}, u32[]{:S(2)}, u32[]{:S(2)}) collective-permute-start(f32[4,4,32]{2,1,0:T(4,128)S(1)} %fusion.267), channel_id=1, source_target_pairs={{0,8},{8,16},{16,24},{1,9},{9,17},{17,25},{2,10},{10,18},{18,26},{... | collective-permute-start | bytes 6152 | tf_op jit(solution)/shard_map/ppermute | solution.py:32
  171.5 1.9 collective-permute-start.39
  173.4 5.9 %collective-permute-start.38 = (f32[12,4,32]{2,1,0:T(4,128)S(1)}, f32[12,4,32]{2,1,0:T(4,128)S(1)}, u32[]{:S(2)}, u32[]{:S(2)}) collective-permute-start(f32[12,4,32]{2,1,0:T(4,128)S(1)} %pad_maximum_fusion.23), channel_id=1, source_target_pairs={{0,2},{2,4},{4,6},{1,3},{3,5},{5,7},{8,10},{10,12},{12,14},{9,11},... | collective-permute-start | bytes 18440 | tf_op jit(solution)/shard_map/ppermute | solution.py:32
  180.3 4.0 %collective-permute-start.40 = (f32[12,12,4]{2,1,0:T(8,128)S(1)}, f32[12,12,4]{2,1,0:T(8,128)S(1)}, u32[]{:S(2)}, u32[]{:S(2)}) collective-permute-start(f32[12,12,4]{2,1,0:T(8,128)S(1)} %get-tuple-element.81), channel_id=1, source_target_pairs={{0,1},{2,3},{4,5},{6,7},{8,9},{10,11},{12,13},{14,15},{16,17},{18,... | collective-permute-start | bytes 6920 | tf_op jit(solution)/shard_map/ppermute | solution.py:32
  186.0 3.7 %collective-permute-done.41 = f32[12,12,4]{2,1,0:T(8,128)S(1)} collective-permute-done((f32[12,12,4]{2,1,0:T(8,128)S(1)}, f32[12,12,4]{2,1,0:T(8,128)S(1)}, u32[]{:S(2)}, u32[]{:S(2)}) %collective-permute-start.41) | collective-permute-done | bytes 2336 | tf_op jit(solution)/shard_map/ppermute | solution.py:33
  191.6 3.9 %collective-permute-start.42 = (f32[2,8,64]{2,1,0:T(8,128)S(1)}, f32[2,8,64]{2,1,0:T(8,128)S(1)}, u32[]{:S(2)}, u32[]{:S(2)}) collective-permute-start(f32[2,8,64]{2,1,0:T(8,128)S(1)} %get-tuple-element.103), channel_id=1, source_target_pairs={{0,8},{8,16},{16,24},{1,9},{9,17},{17,25},{2,10},{10,18},{18,26},{... | collective-permute-start | bytes 12296 | tf_op jit(solution)/shard_map/ppermute | solution.py:32
  196.9 3.4 %collective-permute-done.43 = f32[2,8,64]{2,1,0:T(8,128)S(1)} collective-permute-done((f32[2,8,64]{2,1,0:T(8,128)S(1)}, f32[2,8,64]{2,1,0:T(8,128)S(1)}, u32[]{:S(2)}, u32[]{:S(2)}) %collective-permute-start.43) | collective-permute-done | bytes 4128 | tf_op jit(solution)/shard_map/ppermute | solution.py:33
  200.2 6.8 %collective-permute-start.44 = (f32[12,2,64]{2,1,0:T(2,128)S(1)}, f32[12,2,64]{2,1,0:T(2,128)S(1)}, u32[]{:S(2)}, u32[]{:S(2)}) collective-permute-start(f32[12,2,64]{2,1,0:T(2,128)S(1)} %get-tuple-element.95), channel_id=1, source_target_pairs={{0,2},{2,4},{4,6},{1,3},{3,5},{5,7},{8,10},{10,12},{12,14},{9,11},... | collective-permute-start | bytes 18440 | tf_op jit(solution)/shard_map/ppermute | solution.py:32
  207.0 1.9 collective-permute-start.45
  209.0 3.1 %collective-permute-done.45 = f32[12,2,64]{2,1,0:T(2,128)S(1)} collective-permute-done((f32[12,2,64]{2,1,0:T(2,128)S(1)}, f32[12,2,64]{2,1,0:T(2,128)S(1)}, u32[]{:S(2)}, u32[]{:S(2)}) %collective-permute-start.45) | collective-permute-done | bytes 6176 | tf_op jit(solution)/shard_map/ppermute | solution.py:33
  215.1 3.7 %collective-permute-done.47 = f32[12,12,2]{2,1,0:T(8,128)S(1)} collective-permute-done((f32[12,12,2]{2,1,0:T(8,128)S(1)}, f32[12,12,2]{2,1,0:T(8,128)S(1)}, u32[]{:S(2)}, u32[]{:S(2)}) %collective-permute-start.47) | collective-permute-done | bytes 1184 | tf_op jit(solution)/shard_map/ppermute | solution.py:33
  219.6 3.6 %collective-permute-start.48 = (f32[2,8,64]{2,1,0:T(8,128)S(1)}, f32[2,8,64]{2,1,0:T(8,128)S(1)}, u32[]{:S(2)}, u32[]{:S(2)}) collective-permute-start(f32[2,8,64]{2,1,0:T(8,128)S(1)} %get-tuple-element.101), channel_id=1, source_target_pairs={{0,8},{8,16},{16,24},{1,9},{9,17},{17,25},{2,10},{10,18},{18,26},{... | collective-permute-start | bytes 12296 | tf_op jit(solution)/shard_map/ppermute | solution.py:32
  224.5 3.1 %collective-permute-done.49 = f32[2,8,64]{2,1,0:T(8,128)S(1)} collective-permute-done((f32[2,8,64]{2,1,0:T(8,128)S(1)}, f32[2,8,64]{2,1,0:T(8,128)S(1)}, u32[]{:S(2)}, u32[]{:S(2)}) %collective-permute-start.49) | collective-permute-done | bytes 4128 | tf_op jit(solution)/shard_map/ppermute | solution.py:33
  227.6 4.8 %collective-permute-start.50 = (f32[12,2,64]{2,1,0:T(2,128)S(1)}, f32[12,2,64]{2,1,0:T(2,128)S(1)}, u32[]{:S(2)}, u32[]{:S(2)}) collective-permute-start(f32[12,2,64]{2,1,0:T(2,128)S(1)} %get-tuple-element.93), channel_id=1, source_target_pairs={{0,2},{2,4},{4,6},{1,3},{3,5},{5,7},{8,10},{10,12},{12,14},{9,11},... | collective-permute-start | bytes 18440 | tf_op jit(solution)/shard_map/ppermute | solution.py:32
  232.4 1.9 collective-permute-start.51
  234.3 3.1 %collective-permute-done.51 = f32[12,2,64]{2,1,0:T(2,128)S(1)} collective-permute-done((f32[12,2,64]{2,1,0:T(2,128)S(1)}, f32[12,2,64]{2,1,0:T(2,128)S(1)}, u32[]{:S(2)}, u32[]{:S(2)}) %collective-permute-start.51) | collective-permute-done | bytes 6176 | tf_op jit(solution)/shard_map/ppermute | solution.py:33
  240.4 3.7 %collective-permute-done.53 = f32[12,12,2]{2,1,0:T(8,128)S(1)} collective-permute-done((f32[12,12,2]{2,1,0:T(8,128)S(1)}, f32[12,12,2]{2,1,0:T(8,128)S(1)}, u32[]{:S(2)}, u32[]{:S(2)}) %collective-permute-start.53) | collective-permute-done | bytes 1184 | tf_op jit(solution)/shard_map/ppermute | solution.py:33
  246.6 1.6 collective-permute-start.54
  249.5 3.2 %collective-permute-done.55 = f32[2,16,128]{2,1,0:T(8,128)S(1)} collective-permute-done((f32[2,16,128]{2,1,0:T(8,128)S(1)}, f32[2,16,128]{2,1,0:T(8,128)S(1)}, u32[]{:S(2)}, u32[]{:S(2)}) %collective-permute-start.55) | collective-permute-done | bytes 16416 | tf_op jit(solution)/shard_map/ppermute | solution.py:33
  252.7 4.8 %collective-permute-start.56 = (f32[20,2,128]{2,1,0:T(2,128)S(1)}, f32[20,2,128]{2,1,0:T(2,128)S(1)}, u32[]{:S(2)}, u32[]{:S(2)}) collective-permute-start(f32[20,2,128]{2,1,0:T(2,128)S(1)} %get-tuple-element.47), channel_id=1, source_target_pairs={{0,2},{2,4},{4,6},{1,3},{3,5},{5,7},{8,10},{10,12},{12,14},{9,11},... | collective-permute-start | bytes 61448 | tf_op jit(solution)/shard_map/ppermute | solution.py:32
  257.5 1.9 collective-permute-start.57
  259.4 3.2 %collective-permute-done.57 = f32[20,2,128]{2,1,0:T(2,128)S(1)} collective-permute-done((f32[20,2,128]{2,1,0:T(2,128)S(1)}, f32[20,2,128]{2,1,0:T(2,128)S(1)}, u32[]{:S(2)}, u32[]{:S(2)}) %collective-permute-start.57) | collective-permute-done | bytes 20512 | tf_op jit(solution)/shard_map/ppermute | solution.py:33
  265.4 2.9 %collective-permute-done.58 = f32[20,20,2]{2,1,0:T(8,128)S(1)} collective-permute-done((f32[20,20,2]{2,1,0:T(8,128)S(1)}, f32[20,20,2]{2,1,0:T(8,128)S(1)}, u32[]{:S(2)}, u32[]{:S(2)}) %collective-permute-start.58) | collective-permute-done | bytes 3232 | tf_op jit(solution)/shard_map/ppermute | solution.py:32
  268.2 4.1 %collective-permute-done.59 = f32[20,20,2]{2,1,0:T(8,128)S(1)} collective-permute-done((f32[20,20,2]{2,1,0:T(8,128)S(1)}, f32[20,20,2]{2,1,0:T(8,128)S(1)}, u32[]{:S(2)}, u32[]{:S(2)}) %collective-permute-start.59) | collective-permute-done | bytes 3232 | tf_op jit(solution)/shard_map/ppermute | solution.py:33
  (206 shorter events, 58.3 us)
Async XLA Ops:
  0.0 7.6 %copy-start = (f32[16,16,128]{2,1,0:T(8,128)S(1)}, f32[16,16,128]{2,1,0:T(8,128)}, u32[]{:S(2)}) copy-start(f32[16,16,128]{2,1,0:T(8,128)} %param.2) | copy-start | bytes 393220
  0.8 6.8 %collective-permute-start.1 = (f32[2,16,128]{2,1,0:T(8,128)S(1)}, f32[2,16,128]{2,1,0:T(8,128)S(1)}, u32[]{:S(2)}, u32[]{:S(2)}) collective-permute-start(f32[2,16,128]{2,1,0:T(8,128)S(1)} %get-tuple-element.61), channel_id=1, source_target_pairs={{8,0},{16,8},{24,16},{9,1},{17,9},{25,17},{10,2},{18,10},{26,18},{... | collective-permute-start | bytes 49160 | tf_op jit(solution)/shard_map/ppermute | solution.py:33
  2.1 5.5 %collective-permute-start = (f32[2,16,128]{2,1,0:T(8,128)S(1)}, f32[2,16,128]{2,1,0:T(8,128)S(1)}, u32[]{:S(2)}, u32[]{:S(2)}) collective-permute-start(f32[2,16,128]{2,1,0:T(8,128)S(1)} %get-tuple-element.62), channel_id=1, source_target_pairs={{0,8},{8,16},{16,24},{1,9},{9,17},{17,25},{2,10},{10,18},{18,26},{... | collective-permute-start | bytes 49160 | tf_op jit(solution)/shard_map/ppermute | solution.py:32
  7.7 7.0 %collective-permute-start.2 = (f32[20,2,128]{2,1,0:T(2,128)S(1)}, f32[20,2,128]{2,1,0:T(2,128)S(1)}, u32[]{:S(2)}, u32[]{:S(2)}) collective-permute-start(f32[20,2,128]{2,1,0:T(2,128)S(1)} %get-tuple-element.53), channel_id=1, source_target_pairs={{0,2},{2,4},{4,6},{1,3},{3,5},{5,7},{8,10},{10,12},{12,14},{9,11},... | collective-permute-start | bytes 61448 | tf_op jit(solution)/shard_map/ppermute | solution.py:32
  12.7 5.1 %collective-permute-start.3 = (f32[20,2,128]{2,1,0:T(2,128)S(1)}, f32[20,2,128]{2,1,0:T(2,128)S(1)}, u32[]{:S(2)}, u32[]{:S(2)}) collective-permute-start(f32[20,2,128]{2,1,0:T(2,128)S(1)} %get-tuple-element.54), channel_id=1, source_target_pairs={{2,0},{4,2},{6,4},{3,1},{5,3},{7,5},{10,8},{12,10},{14,12},{11,9},... | collective-permute-start | bytes 61448 | tf_op jit(solution)/shard_map/ppermute | solution.py:33
  17.9 7.3 %collective-permute-start.4 = (f32[20,20,2]{2,1,0:T(8,128)S(1)}, f32[20,20,2]{2,1,0:T(8,128)S(1)}, u32[]{:S(2)}, u32[]{:S(2)}) collective-permute-start(f32[20,20,2]{2,1,0:T(8,128)S(1)} %get-tuple-element.37), channel_id=1, source_target_pairs={{0,1},{2,3},{4,5},{6,7},{8,9},{10,11},{12,13},{14,15},{16,17},{18,... | collective-permute-start | bytes 9608 | tf_op jit(solution)/shard_map/ppermute | solution.py:32
  21.1 8.3 %collective-permute-start.5 = (f32[20,20,2]{2,1,0:T(8,128)S(1)}, f32[20,20,2]{2,1,0:T(8,128)S(1)}, u32[]{:S(2)}, u32[]{:S(2)}) collective-permute-start(f32[20,20,2]{2,1,0:T(8,128)S(1)} %get-tuple-element.38), channel_id=1, source_target_pairs={{1,0},{3,2},{5,4},{7,6},{9,8},{11,10},{13,12},{15,14},{17,16},{19,... | collective-permute-start | bytes 9608 | tf_op jit(solution)/shard_map/ppermute | solution.py:33
  30.0 0.9 copy-start.1
  31.1 5.2 %collective-permute-start.6 = (f32[2,16,128]{2,1,0:T(8,128)S(1)}, f32[2,16,128]{2,1,0:T(8,128)S(1)}, u32[]{:S(2)}, u32[]{:S(2)}) collective-permute-start(f32[2,16,128]{2,1,0:T(8,128)S(1)} %get-tuple-element.59), channel_id=1, source_target_pairs={{0,8},{8,16},{16,24},{1,9},{9,17},{17,25},{2,10},{10,18},{18,26},{... | collective-permute-start | bytes 49160 | tf_op jit(solution)/shard_map/ppermute | solution.py:32
  35.0 4.8 %collective-permute-start.7 = (f32[2,16,128]{2,1,0:T(8,128)S(1)}, f32[2,16,128]{2,1,0:T(8,128)S(1)}, u32[]{:S(2)}, u32[]{:S(2)}) collective-permute-start(f32[2,16,128]{2,1,0:T(8,128)S(1)} %get-tuple-element.60), channel_id=1, source_target_pairs={{8,0},{16,8},{24,16},{9,1},{17,9},{25,17},{10,2},{18,10},{26,18},{... | collective-permute-start | bytes 49160 | tf_op jit(solution)/shard_map/ppermute | solution.py:33
  39.8 5.1 %collective-permute-start.8 = (f32[20,2,128]{2,1,0:T(2,128)S(1)}, f32[20,2,128]{2,1,0:T(2,128)S(1)}, u32[]{:S(2)}, u32[]{:S(2)}) collective-permute-start(f32[20,2,128]{2,1,0:T(2,128)S(1)} %get-tuple-element.51), channel_id=1, source_target_pairs={{0,2},{2,4},{4,6},{1,3},{3,5},{5,7},{8,10},{10,12},{12,14},{9,11},... | collective-permute-start | bytes 61448 | tf_op jit(solution)/shard_map/ppermute | solution.py:32
  42.9 5.1 %collective-permute-start.9 = (f32[20,2,128]{2,1,0:T(2,128)S(1)}, f32[20,2,128]{2,1,0:T(2,128)S(1)}, u32[]{:S(2)}, u32[]{:S(2)}) collective-permute-start(f32[20,2,128]{2,1,0:T(2,128)S(1)} %get-tuple-element.52), channel_id=1, source_target_pairs={{2,0},{4,2},{6,4},{3,1},{5,3},{7,5},{10,8},{12,10},{14,12},{11,9},... | collective-permute-start | bytes 61448 | tf_op jit(solution)/shard_map/ppermute | solution.py:33
  48.2 5.4 %collective-permute-start.10 = (f32[20,20,2]{2,1,0:T(8,128)S(1)}, f32[20,20,2]{2,1,0:T(8,128)S(1)}, u32[]{:S(2)}, u32[]{:S(2)}) collective-permute-start(f32[20,20,2]{2,1,0:T(8,128)S(1)} %get-tuple-element.35), channel_id=1, source_target_pairs={{0,1},{2,3},{4,5},{6,7},{8,9},{10,11},{12,13},{14,15},{16,17},{18,... | collective-permute-start | bytes 9608 | tf_op jit(solution)/shard_map/ppermute | solution.py:32
  49.5 8.2 %collective-permute-start.11 = (f32[20,20,2]{2,1,0:T(8,128)S(1)}, f32[20,20,2]{2,1,0:T(8,128)S(1)}, u32[]{:S(2)}, u32[]{:S(2)}) collective-permute-start(f32[20,20,2]{2,1,0:T(8,128)S(1)} %get-tuple-element.36), channel_id=1, source_target_pairs={{1,0},{3,2},{5,4},{7,6},{9,8},{11,10},{13,12},{15,14},{17,16},{19,... | collective-permute-start | bytes 9608 | tf_op jit(solution)/shard_map/ppermute | solution.py:33
  59.0 4.5 %collective-permute-start.12 = (f32[2,16,128]{2,1,0:T(8,128)S(1)}, f32[2,16,128]{2,1,0:T(8,128)S(1)}, u32[]{:S(2)}, u32[]{:S(2)}) collective-permute-start(f32[2,16,128]{2,1,0:T(8,128)S(1)} %get-tuple-element.57), channel_id=1, source_target_pairs={{0,8},{8,16},{16,24},{1,9},{9,17},{17,25},{2,10},{10,18},{18,26},{... | collective-permute-start | bytes 49160 | tf_op jit(solution)/shard_map/ppermute | solution.py:32
  62.3 4.9 %collective-permute-start.13 = (f32[2,16,128]{2,1,0:T(8,128)S(1)}, f32[2,16,128]{2,1,0:T(8,128)S(1)}, u32[]{:S(2)}, u32[]{:S(2)}) collective-permute-start(f32[2,16,128]{2,1,0:T(8,128)S(1)} %get-tuple-element.58), channel_id=1, source_target_pairs={{8,0},{16,8},{24,16},{9,1},{17,9},{25,17},{10,2},{18,10},{26,18},{... | collective-permute-start | bytes 49160 | tf_op jit(solution)/shard_map/ppermute | solution.py:33
  67.2 4.9 %collective-permute-start.14 = (f32[20,2,128]{2,1,0:T(2,128)S(1)}, f32[20,2,128]{2,1,0:T(2,128)S(1)}, u32[]{:S(2)}, u32[]{:S(2)}) collective-permute-start(f32[20,2,128]{2,1,0:T(2,128)S(1)} %get-tuple-element.49), channel_id=1, source_target_pairs={{0,2},{2,4},{4,6},{1,3},{3,5},{5,7},{8,10},{10,12},{12,14},{9,11},... | collective-permute-start | bytes 61448 | tf_op jit(solution)/shard_map/ppermute | solution.py:32
  70.2 5.1 %collective-permute-start.15 = (f32[20,2,128]{2,1,0:T(2,128)S(1)}, f32[20,2,128]{2,1,0:T(2,128)S(1)}, u32[]{:S(2)}, u32[]{:S(2)}) collective-permute-start(f32[20,2,128]{2,1,0:T(2,128)S(1)} %get-tuple-element.50), channel_id=1, source_target_pairs={{2,0},{4,2},{6,4},{3,1},{5,3},{7,5},{10,8},{12,10},{14,12},{11,9},... | collective-permute-start | bytes 61448 | tf_op jit(solution)/shard_map/ppermute | solution.py:33
  75.5 5.4 %collective-permute-start.16 = (f32[20,20,2]{2,1,0:T(8,128)S(1)}, f32[20,20,2]{2,1,0:T(8,128)S(1)}, u32[]{:S(2)}, u32[]{:S(2)}) collective-permute-start(f32[20,20,2]{2,1,0:T(8,128)S(1)} %get-tuple-element.33), channel_id=1, source_target_pairs={{0,1},{2,3},{4,5},{6,7},{8,9},{10,11},{12,13},{14,15},{16,17},{18,... | collective-permute-start | bytes 9608 | tf_op jit(solution)/shard_map/ppermute | solution.py:32
  76.8 8.2 %collective-permute-start.17 = (f32[20,20,2]{2,1,0:T(8,128)S(1)}, f32[20,20,2]{2,1,0:T(8,128)S(1)}, u32[]{:S(2)}, u32[]{:S(2)}) collective-permute-start(f32[20,20,2]{2,1,0:T(8,128)S(1)} %get-tuple-element.34), channel_id=1, source_target_pairs={{1,0},{3,2},{5,4},{7,6},{9,8},{11,10},{13,12},{15,14},{17,16},{19,... | collective-permute-start | bytes 9608 | tf_op jit(solution)/shard_map/ppermute | solution.py:33
  86.2 4.1 %collective-permute-start.18 = (f32[3,16,128]{2,1,0:T(8,128)S(1)}, f32[3,16,128]{2,1,0:T(8,128)S(1)}, u32[]{:S(2)}, u32[]{:S(2)}) collective-permute-start(f32[3,16,128]{2,1,0:T(8,128)S(1)} %slice.1422), channel_id=1, source_target_pairs={{0,8},{8,16},{16,24},{1,9},{9,17},{17,25},{2,10},{10,18},{18,26},{... | collective-permute-start | bytes 73736 | tf_op jit(solution)/shard_map/ppermute | solution.py:41
  90.4 3.9 %collective-permute-start.19 = (f32[19,3,128]{2,1,0:T(4,128)S(1)}, f32[19,3,128]{2,1,0:T(4,128)S(1)}, u32[]{:S(2)}, u32[]{:S(2)}) collective-permute-start(f32[19,3,128]{2,1,0:T(4,128)S(1)} %pad_maximum_fusion.22), channel_id=1, source_target_pairs={{0,2},{2,4},{4,6},{1,3},{3,5},{5,7},{8,10},{10,12},{12,14},{9,11},... | collective-permute-start | bytes 87560 | tf_op jit(solution)/shard_map/ppermute | solution.py:41
  94.5 6.8 %collective-permute-start.20 = (f32[19,19,3]{2,1,0:T(8,128)S(1)}, f32[19,19,3]{2,1,0:T(8,128)S(1)}, u32[]{:S(2)}, u32[]{:S(2)}) collective-permute-start(f32[19,19,3]{2,1,0:T(8,128)S(1)} %pad_maximum_fusion.8), channel_id=1, source_target_pairs={{0,1},{2,3},{4,5},{6,7},{8,9},{10,11},{12,13},{14,15},{16,17},{18,... | collective-permute-start | bytes 13004 | tf_op jit(solution)/shard_map/ppermute | solution.py:41
  102.5 5.0 %collective-permute-start.21 = (f32[2,8,64]{2,1,0:T(8,128)S(1)}, f32[2,8,64]{2,1,0:T(8,128)S(1)}, u32[]{:S(2)}, u32[]{:S(2)}) collective-permute-start(f32[2,8,64]{2,1,0:T(8,128)S(1)} %get-tuple-element.107), channel_id=1, source_target_pairs={{0,8},{8,16},{16,24},{1,9},{9,17},{17,25},{2,10},{10,18},{18,26},{... | collective-permute-start | bytes 12296 | tf_op jit(solution)/shard_map/ppermute | solution.py:32
  106.2 4.4 %collective-permute-start.22 = (f32[2,8,64]{2,1,0:T(8,128)S(1)}, f32[2,8,64]{2,1,0:T(8,128)S(1)}, u32[]{:S(2)}, u32[]{:S(2)}) collective-permute-start(f32[2,8,64]{2,1,0:T(8,128)S(1)} %get-tuple-element.108), channel_id=1, source_target_pairs={{8,0},{16,8},{24,16},{9,1},{17,9},{25,17},{10,2},{18,10},{26,18},{... | collective-permute-start | bytes 12296 | tf_op jit(solution)/shard_map/ppermute | solution.py:33
  110.6 6.1 %collective-permute-start.23 = (f32[12,2,64]{2,1,0:T(2,128)S(1)}, f32[12,2,64]{2,1,0:T(2,128)S(1)}, u32[]{:S(2)}, u32[]{:S(2)}) collective-permute-start(f32[12,2,64]{2,1,0:T(2,128)S(1)} %get-tuple-element.99), channel_id=1, source_target_pairs={{0,2},{2,4},{4,6},{1,3},{3,5},{5,7},{8,10},{10,12},{12,14},{9,11},... | collective-permute-start | bytes 18440 | tf_op jit(solution)/shard_map/ppermute | solution.py:32
  114.8 5.0 %collective-permute-start.24 = (f32[12,2,64]{2,1,0:T(2,128)S(1)}, f32[12,2,64]{2,1,0:T(2,128)S(1)}, u32[]{:S(2)}, u32[]{:S(2)}) collective-permute-start(f32[12,2,64]{2,1,0:T(2,128)S(1)} %get-tuple-element.100), channel_id=1, source_target_pairs={{2,0},{4,2},{6,4},{3,1},{5,3},{7,5},{10,8},{12,10},{14,12},{11,9},... | collective-permute-start | bytes 18440 | tf_op jit(solution)/shard_map/ppermute | solution.py:33
  119.9 5.7 %collective-permute-start.25 = (f32[12,12,2]{2,1,0:T(8,128)S(1)}, f32[12,12,2]{2,1,0:T(8,128)S(1)}, u32[]{:S(2)}, u32[]{:S(2)}) collective-permute-start(f32[12,12,2]{2,1,0:T(8,128)S(1)} %get-tuple-element.85), channel_id=1, source_target_pairs={{0,1},{2,3},{4,5},{6,7},{8,9},{10,11},{12,13},{14,15},{16,17},{18,... | collective-permute-start | bytes 3464 | tf_op jit(solution)/shard_map/ppermute | solution.py:32
  124.0 5.4 %collective-permute-start.26 = (f32[12,12,2]{2,1,0:T(8,128)S(1)}, f32[12,12,2]{2,1,0:T(8,128)S(1)}, u32[]{:S(2)}, u32[]{:S(2)}) collective-permute-start(f32[12,12,2]{2,1,0:T(8,128)S(1)} %get-tuple-element.86), channel_id=1, source_target_pairs={{1,0},{3,2},{5,4},{7,6},{9,8},{11,10},{13,12},{15,14},{17,16},{19,... | collective-permute-start | bytes 3464 | tf_op jit(solution)/shard_map/ppermute | solution.py:33
  130.1 3.0 %collective-permute-start.27 = (f32[2,8,64]{2,1,0:T(8,128)S(1)}, f32[2,8,64]{2,1,0:T(8,128)S(1)}, u32[]{:S(2)}, u32[]{:S(2)}) collective-permute-start(f32[2,8,64]{2,1,0:T(8,128)S(1)} %get-tuple-element.105), channel_id=1, source_target_pairs={{0,8},{8,16},{16,24},{1,9},{9,17},{17,25},{2,10},{10,18},{18,26},{... | collective-permute-start | bytes 12296 | tf_op jit(solution)/shard_map/ppermute | solution.py:32
  131.8 4.4 %collective-permute-start.28 = (f32[2,8,64]{2,1,0:T(8,128)S(1)}, f32[2,8,64]{2,1,0:T(8,128)S(1)}, u32[]{:S(2)}, u32[]{:S(2)}) collective-permute-start(f32[2,8,64]{2,1,0:T(8,128)S(1)} %get-tuple-element.106), channel_id=1, source_target_pairs={{8,0},{16,8},{24,16},{9,1},{17,9},{25,17},{10,2},{18,10},{26,18},{... | collective-permute-start | bytes 12296 | tf_op jit(solution)/shard_map/ppermute | solution.py:33
  136.2 6.8 %collective-permute-start.29 = (f32[12,2,64]{2,1,0:T(2,128)S(1)}, f32[12,2,64]{2,1,0:T(2,128)S(1)}, u32[]{:S(2)}, u32[]{:S(2)}) collective-permute-start(f32[12,2,64]{2,1,0:T(2,128)S(1)} %get-tuple-element.97), channel_id=1, source_target_pairs={{0,2},{2,4},{4,6},{1,3},{3,5},{5,7},{8,10},{10,12},{12,14},{9,11},... | collective-permute-start | bytes 18440 | tf_op jit(solution)/shard_map/ppermute | solution.py:32
  141.0 5.0 %collective-permute-start.30 = (f32[12,2,64]{2,1,0:T(2,128)S(1)}, f32[12,2,64]{2,1,0:T(2,128)S(1)}, u32[]{:S(2)}, u32[]{:S(2)}) collective-permute-start(f32[12,2,64]{2,1,0:T(2,128)S(1)} %get-tuple-element.98), channel_id=1, source_target_pairs={{2,0},{4,2},{6,4},{3,1},{5,3},{7,5},{10,8},{12,10},{14,12},{11,9},... | collective-permute-start | bytes 18440 | tf_op jit(solution)/shard_map/ppermute | solution.py:33
  146.1 2.9 %collective-permute-start.31 = (f32[12,12,2]{2,1,0:T(8,128)S(1)}, f32[12,12,2]{2,1,0:T(8,128)S(1)}, u32[]{:S(2)}, u32[]{:S(2)}) collective-permute-start(f32[12,12,2]{2,1,0:T(8,128)S(1)} %get-tuple-element.83), channel_id=1, source_target_pairs={{0,1},{2,3},{4,5},{6,7},{8,9},{10,11},{12,13},{14,15},{16,17},{18,... | collective-permute-start | bytes 3464 | tf_op jit(solution)/shard_map/ppermute | solution.py:32
  147.4 5.4 %collective-permute-start.32 = (f32[12,12,2]{2,1,0:T(8,128)S(1)}, f32[12,12,2]{2,1,0:T(8,128)S(1)}, u32[]{:S(2)}, u32[]{:S(2)}) collective-permute-start(f32[12,12,2]{2,1,0:T(8,128)S(1)} %get-tuple-element.84), channel_id=1, source_target_pairs={{1,0},{3,2},{5,4},{7,6},{9,8},{11,10},{13,12},{15,14},{17,16},{19,... | collective-permute-start | bytes 3464 | tf_op jit(solution)/shard_map/ppermute | solution.py:33
  153.5 2.5 collective-permute-start.33
  156.0 5.1 %collective-permute-start.34 = (f32[11,3,64]{2,1,0:T(4,128)S(1)}, f32[11,3,64]{2,1,0:T(4,128)S(1)}, u32[]{:S(2)}, u32[]{:S(2)}) collective-permute-start(f32[11,3,64]{2,1,0:T(4,128)S(1)} %pad_maximum_fusion.24), channel_id=1, source_target_pairs={{0,2},{2,4},{4,6},{1,3},{3,5},{5,7},{8,10},{10,12},{12,14},{9,11},... | collective-permute-start | bytes 25352 | tf_op jit(solution)/shard_map/ppermute | solution.py:41
  161.2 2.8 %collective-permute-start.35 = (f32[11,11,3]{2,1,0:T(8,128)S(1)}, f32[11,11,3]{2,1,0:T(8,128)S(1)}, u32[]{:S(2)}, u32[]{:S(2)}) collective-permute-start(f32[11,11,3]{2,1,0:T(8,128)S(1)} %pad_maximum_fusion.20), channel_id=1, source_target_pairs={{0,1},{2,3},{4,5},{6,7},{8,9},{10,11},{12,13},{14,15},{16,17},{18,... | collective-permute-start | bytes 4364 | tf_op jit(solution)/shard_map/ppermute | solution.py:41
  164.8 5.9 %collective-permute-start.37 = (f32[4,4,32]{2,1,0:T(4,128)S(1)}, f32[4,4,32]{2,1,0:T(4,128)S(1)}, u32[]{:S(2)}, u32[]{:S(2)}) collective-permute-start(f32[4,4,32]{2,1,0:T(4,128)S(1)} %fusion.267), channel_id=1, source_target_pairs={{8,0},{16,8},{24,16},{9,1},{17,9},{25,17},{10,2},{18,10},{26,18},{... | collective-permute-start | bytes 6152 | tf_op jit(solution)/shard_map/ppermute | solution.py:33
  166.1 5.3 %collective-permute-start.36 = (f32[4,4,32]{2,1,0:T(4,128)S(1)}, f32[4,4,32]{2,1,0:T(4,128)S(1)}, u32[]{:S(2)}, u32[]{:S(2)}) collective-permute-start(f32[4,4,32]{2,1,0:T(4,128)S(1)} %fusion.267), channel_id=1, source_target_pairs={{0,8},{8,16},{16,24},{1,9},{9,17},{17,25},{2,10},{10,18},{18,26},{... | collective-permute-start | bytes 6152 | tf_op jit(solution)/shard_map/ppermute | solution.py:32
  171.5 7.8 %collective-permute-start.39 = (f32[12,4,32]{2,1,0:T(4,128)S(1)}, f32[12,4,32]{2,1,0:T(4,128)S(1)}, u32[]{:S(2)}, u32[]{:S(2)}) collective-permute-start(f32[12,4,32]{2,1,0:T(4,128)S(1)} %pad_maximum_fusion.23), channel_id=1, source_target_pairs={{2,0},{4,2},{6,4},{3,1},{5,3},{7,5},{10,8},{12,10},{14,12},{11,9},... | collective-permute-start | bytes 18440 | tf_op jit(solution)/shard_map/ppermute | solution.py:33
  173.4 6.8 %collective-permute-start.38 = (f32[12,4,32]{2,1,0:T(4,128)S(1)}, f32[12,4,32]{2,1,0:T(4,128)S(1)}, u32[]{:S(2)}, u32[]{:S(2)}) collective-permute-start(f32[12,4,32]{2,1,0:T(4,128)S(1)} %pad_maximum_fusion.23), channel_id=1, source_target_pairs={{0,2},{2,4},{4,6},{1,3},{3,5},{5,7},{8,10},{10,12},{12,14},{9,11},... | collective-permute-start | bytes 18440 | tf_op jit(solution)/shard_map/ppermute | solution.py:32
  180.3 5.6 %collective-permute-start.40 = (f32[12,12,4]{2,1,0:T(8,128)S(1)}, f32[12,12,4]{2,1,0:T(8,128)S(1)}, u32[]{:S(2)}, u32[]{:S(2)}) collective-permute-start(f32[12,12,4]{2,1,0:T(8,128)S(1)} %get-tuple-element.81), channel_id=1, source_target_pairs={{0,1},{2,3},{4,5},{6,7},{8,9},{10,11},{12,13},{14,15},{16,17},{18,... | collective-permute-start | bytes 6920 | tf_op jit(solution)/shard_map/ppermute | solution.py:32
  184.3 5.4 %collective-permute-start.41 = (f32[12,12,4]{2,1,0:T(8,128)S(1)}, f32[12,12,4]{2,1,0:T(8,128)S(1)}, u32[]{:S(2)}, u32[]{:S(2)}) collective-permute-start(f32[12,12,4]{2,1,0:T(8,128)S(1)} %get-tuple-element.82), channel_id=1, source_target_pairs={{1,0},{3,2},{5,4},{7,6},{9,8},{11,10},{13,12},{15,14},{17,16},{19,... | collective-permute-start | bytes 6920 | tf_op jit(solution)/shard_map/ppermute | solution.py:33
  191.6 5.2 %collective-permute-start.42 = (f32[2,8,64]{2,1,0:T(8,128)S(1)}, f32[2,8,64]{2,1,0:T(8,128)S(1)}, u32[]{:S(2)}, u32[]{:S(2)}) collective-permute-start(f32[2,8,64]{2,1,0:T(8,128)S(1)} %get-tuple-element.103), channel_id=1, source_target_pairs={{0,8},{8,16},{16,24},{1,9},{9,17},{17,25},{2,10},{10,18},{18,26},{... | collective-permute-start | bytes 12296 | tf_op jit(solution)/shard_map/ppermute | solution.py:32
  195.5 4.7 %collective-permute-start.43 = (f32[2,8,64]{2,1,0:T(8,128)S(1)}, f32[2,8,64]{2,1,0:T(8,128)S(1)}, u32[]{:S(2)}, u32[]{:S(2)}) collective-permute-start(f32[2,8,64]{2,1,0:T(8,128)S(1)} %get-tuple-element.104), channel_id=1, source_target_pairs={{8,0},{16,8},{24,16},{9,1},{17,9},{25,17},{10,2},{18,10},{26,18},{... | collective-permute-start | bytes 12296 | tf_op jit(solution)/shard_map/ppermute | solution.py:33
  200.2 8.7 %collective-permute-start.44 = (f32[12,2,64]{2,1,0:T(2,128)S(1)}, f32[12,2,64]{2,1,0:T(2,128)S(1)}, u32[]{:S(2)}, u32[]{:S(2)}) collective-permute-start(f32[12,2,64]{2,1,0:T(2,128)S(1)} %get-tuple-element.95), channel_id=1, source_target_pairs={{0,2},{2,4},{4,6},{1,3},{3,5},{5,7},{8,10},{10,12},{12,14},{9,11},... | collective-permute-start | bytes 18440 | tf_op jit(solution)/shard_map/ppermute | solution.py:32
  207.0 5.0 %collective-permute-start.45 = (f32[12,2,64]{2,1,0:T(2,128)S(1)}, f32[12,2,64]{2,1,0:T(2,128)S(1)}, u32[]{:S(2)}, u32[]{:S(2)}) collective-permute-start(f32[12,2,64]{2,1,0:T(2,128)S(1)} %get-tuple-element.96), channel_id=1, source_target_pairs={{2,0},{4,2},{6,4},{3,1},{5,3},{7,5},{10,8},{12,10},{14,12},{11,9},... | collective-permute-start | bytes 18440 | tf_op jit(solution)/shard_map/ppermute | solution.py:33
  212.2 2.9 %collective-permute-start.46 = (f32[12,12,2]{2,1,0:T(8,128)S(1)}, f32[12,12,2]{2,1,0:T(8,128)S(1)}, u32[]{:S(2)}, u32[]{:S(2)}) collective-permute-start(f32[12,12,2]{2,1,0:T(8,128)S(1)} %get-tuple-element.75), channel_id=1, source_target_pairs={{0,1},{2,3},{4,5},{6,7},{8,9},{10,11},{12,13},{14,15},{16,17},{18,... | collective-permute-start | bytes 3464 | tf_op jit(solution)/shard_map/ppermute | solution.py:32
  213.5 5.4 %collective-permute-start.47 = (f32[12,12,2]{2,1,0:T(8,128)S(1)}, f32[12,12,2]{2,1,0:T(8,128)S(1)}, u32[]{:S(2)}, u32[]{:S(2)}) collective-permute-start(f32[12,12,2]{2,1,0:T(8,128)S(1)} %get-tuple-element.76), channel_id=1, source_target_pairs={{1,0},{3,2},{5,4},{7,6},{9,8},{11,10},{13,12},{15,14},{17,16},{19,... | collective-permute-start | bytes 3464 | tf_op jit(solution)/shard_map/ppermute | solution.py:33
  219.6 5.0 %collective-permute-start.48 = (f32[2,8,64]{2,1,0:T(8,128)S(1)}, f32[2,8,64]{2,1,0:T(8,128)S(1)}, u32[]{:S(2)}, u32[]{:S(2)}) collective-permute-start(f32[2,8,64]{2,1,0:T(8,128)S(1)} %get-tuple-element.101), channel_id=1, source_target_pairs={{0,8},{8,16},{16,24},{1,9},{9,17},{17,25},{2,10},{10,18},{18,26},{... | collective-permute-start | bytes 12296 | tf_op jit(solution)/shard_map/ppermute | solution.py:32
  223.2 4.4 %collective-permute-start.49 = (f32[2,8,64]{2,1,0:T(8,128)S(1)}, f32[2,8,64]{2,1,0:T(8,128)S(1)}, u32[]{:S(2)}, u32[]{:S(2)}) collective-permute-start(f32[2,8,64]{2,1,0:T(8,128)S(1)} %get-tuple-element.102), channel_id=1, source_target_pairs={{8,0},{16,8},{24,16},{9,1},{17,9},{25,17},{10,2},{18,10},{26,18},{... | collective-permute-start | bytes 12296 | tf_op jit(solution)/shard_map/ppermute | solution.py:33
  227.6 6.7 %collective-permute-start.50 = (f32[12,2,64]{2,1,0:T(2,128)S(1)}, f32[12,2,64]{2,1,0:T(2,128)S(1)}, u32[]{:S(2)}, u32[]{:S(2)}) collective-permute-start(f32[12,2,64]{2,1,0:T(2,128)S(1)} %get-tuple-element.93), channel_id=1, source_target_pairs={{0,2},{2,4},{4,6},{1,3},{3,5},{5,7},{8,10},{10,12},{12,14},{9,11},... | collective-permute-start | bytes 18440 | tf_op jit(solution)/shard_map/ppermute | solution.py:32
  232.4 5.0 %collective-permute-start.51 = (f32[12,2,64]{2,1,0:T(2,128)S(1)}, f32[12,2,64]{2,1,0:T(2,128)S(1)}, u32[]{:S(2)}, u32[]{:S(2)}) collective-permute-start(f32[12,2,64]{2,1,0:T(2,128)S(1)} %get-tuple-element.94), channel_id=1, source_target_pairs={{2,0},{4,2},{6,4},{3,1},{5,3},{7,5},{10,8},{12,10},{14,12},{11,9},... | collective-permute-start | bytes 18440 | tf_op jit(solution)/shard_map/ppermute | solution.py:33
  237.5 2.9 %collective-permute-start.52 = (f32[12,12,2]{2,1,0:T(8,128)S(1)}, f32[12,12,2]{2,1,0:T(8,128)S(1)}, u32[]{:S(2)}, u32[]{:S(2)}) collective-permute-start(f32[12,12,2]{2,1,0:T(8,128)S(1)} %get-tuple-element.73), channel_id=1, source_target_pairs={{0,1},{2,3},{4,5},{6,7},{8,9},{10,11},{12,13},{14,15},{16,17},{18,... | collective-permute-start | bytes 3464 | tf_op jit(solution)/shard_map/ppermute | solution.py:32
  238.8 5.4 %collective-permute-start.53 = (f32[12,12,2]{2,1,0:T(8,128)S(1)}, f32[12,12,2]{2,1,0:T(8,128)S(1)}, u32[]{:S(2)}, u32[]{:S(2)}) collective-permute-start(f32[12,12,2]{2,1,0:T(8,128)S(1)} %get-tuple-element.74), channel_id=1, source_target_pairs={{1,0},{3,2},{5,4},{7,6},{9,8},{11,10},{13,12},{15,14},{17,16},{19,... | collective-permute-start | bytes 3464 | tf_op jit(solution)/shard_map/ppermute | solution.py:33
  246.6 3.0 %collective-permute-start.54 = (f32[2,16,128]{2,1,0:T(8,128)S(1)}, f32[2,16,128]{2,1,0:T(8,128)S(1)}, u32[]{:S(2)}, u32[]{:S(2)}) collective-permute-start(f32[2,16,128]{2,1,0:T(8,128)S(1)} %get-tuple-element.55), channel_id=1, source_target_pairs={{0,8},{8,16},{16,24},{1,9},{9,17},{17,25},{2,10},{10,18},{18,26},{... | collective-permute-start | bytes 49160 | tf_op jit(solution)/shard_map/ppermute | solution.py:32
  248.2 4.5 %collective-permute-start.55 = (f32[2,16,128]{2,1,0:T(8,128)S(1)}, f32[2,16,128]{2,1,0:T(8,128)S(1)}, u32[]{:S(2)}, u32[]{:S(2)}) collective-permute-start(f32[2,16,128]{2,1,0:T(8,128)S(1)} %get-tuple-element.56), channel_id=1, source_target_pairs={{8,0},{16,8},{24,16},{9,1},{17,9},{25,17},{10,2},{18,10},{26,18},{... | collective-permute-start | bytes 49160 | tf_op jit(solution)/shard_map/ppermute | solution.py:33
  252.7 6.7 %collective-permute-start.56 = (f32[20,2,128]{2,1,0:T(2,128)S(1)}, f32[20,2,128]{2,1,0:T(2,128)S(1)}, u32[]{:S(2)}, u32[]{:S(2)}) collective-permute-start(f32[20,2,128]{2,1,0:T(2,128)S(1)} %get-tuple-element.47), channel_id=1, source_target_pairs={{0,2},{2,4},{4,6},{1,3},{3,5},{5,7},{8,10},{10,12},{12,14},{9,11},... | collective-permute-start | bytes 61448 | tf_op jit(solution)/shard_map/ppermute | solution.py:32
  257.5 5.1 %collective-permute-start.57 = (f32[20,2,128]{2,1,0:T(2,128)S(1)}, f32[20,2,128]{2,1,0:T(2,128)S(1)}, u32[]{:S(2)}, u32[]{:S(2)}) collective-permute-start(f32[20,2,128]{2,1,0:T(2,128)S(1)} %get-tuple-element.48), channel_id=1, source_target_pairs={{2,0},{4,2},{6,4},{3,1},{5,3},{7,5},{10,8},{12,10},{14,12},{11,9},... | collective-permute-start | bytes 61448 | tf_op jit(solution)/shard_map/ppermute | solution.py:33
  262.8 5.5 %collective-permute-start.58 = (f32[20,20,2]{2,1,0:T(8,128)S(1)}, f32[20,20,2]{2,1,0:T(8,128)S(1)}, u32[]{:S(2)}, u32[]{:S(2)}) collective-permute-start(f32[20,20,2]{2,1,0:T(8,128)S(1)} %get-tuple-element.31), channel_id=1, source_target_pairs={{0,1},{2,3},{4,5},{6,7},{8,9},{10,11},{12,13},{14,15},{16,17},{18,... | collective-permute-start | bytes 9608 | tf_op jit(solution)/shard_map/ppermute | solution.py:32
  264.1 8.3 %collective-permute-start.59 = (f32[20,20,2]{2,1,0:T(8,128)S(1)}, f32[20,20,2]{2,1,0:T(8,128)S(1)}, u32[]{:S(2)}, u32[]{:S(2)}) collective-permute-start(f32[20,20,2]{2,1,0:T(8,128)S(1)} %get-tuple-element.32), channel_id=1, source_target_pairs={{1,0},{3,2},{5,4},{7,6},{9,8},{11,10},{13,12},{15,14},{17,16},{19,... | collective-permute-start | bytes 9608 | tf_op jit(solution)/shard_map/ppermute | solution.py:33
where the time goes:
time: 276 us; the launch traced here: 274 us
  starting transfers between devices  147 us (53%)
  waiting for transfers between devices  108 us (39%)
  other arithmetic  11.2 us (4%)
  matrix products  3.92 us (1%)
    ppermute x27, starting transfers between devices, extended_2(): before = lax.ppermute(last, axis, up)  92.1 us
    ppermute x27, waiting for transfers between devices, extended_2(): after = lax.ppermute(leading, axis, down)  82.8 us
    ppermute x27, starting transfers between devices, extended_2(): after = lax.ppermute(leading, axis, down)  40.7 us
    ppermute x27, waiting for transfers between devices, extended_2(): before = lax.ppermute(last, axis, up)  14.6 us
    ppermute x6, starting transfers between devices, from_behind(): return lax.ppermute(value, axis, pairs)  14.5 us
    ppermute x6, waiting for transfers between devices, from_behind(): return lax.ppermute(value, axis, pairs)  10.7 us
  transfers between devices with their start and end apart: 60, of which 42 were waited for; matrix products, arithmetic and copies ran while one was open for 0% of the time, Pallas kernels for 0%

commit v1 on v0

v1 whole, which is shorter than its diff:
```python
import functools

import jax
import jax.numpy as jnp
import numpy as np
from jax import lax
from jax.experimental import pallas as pl
from jax.experimental.pallas import tpu as pltpu
from jax.sharding import PartitionSpec as P

F32 = jnp.float32
BF16 = jnp.bfloat16
MESH = pl.DeviceIdType.MESH
H = 8
ZR = 32
REACH = 3

RHO0 = 1.0 / 1.2
RHO1 = 1.0 / (2.4 - RHO0)
FIRST = 1.0 / 1.32
KEEP = RHO1 * RHO0
STEP = 2.0 * RHO1 / 1.1


def band_matrices(size, cyclic):
    mass = np.zeros((size, size), np.float32)
    stiff = np.zeros((size, size), np.float32)
    for out in range(size):
        if out % 2 == 0:
            taps = ((-2, -1, 1), (-1, 2, -8), (0, 8, 14), (1, 2, -8), (2, -1, 1))
        else:
            taps = ((-1, 2, -8), (0, 16, 16), (1, 2, -8))
        for off, m, k in taps:
            src = out + off
            if cyclic:
                src %= size
            if 0 <= src < size:
                mass[src, out] += m
                stiff[src, out] += k
    return np.concatenate([mass, stiff], axis=1)


def restrict_taps(g):
    if g % 2 == 0:
        return ((-3, -0.125), (-1, 0.375), (0, 1.0), (1, 0.375), (3, -0.125))
    return ((-1, 0.75), (0, 1.0), (1, 0.75))


def prolong_taps(f):
    if f % 2 == 0:
        return ((f // 2, 1.0),)
    q = f // 4
    if f % 4 == 1:
        return ((2 * q, 0.375), (2 * q + 1, 0.75), (2 * q + 2, -0.125))
    return ((2 * q, -0.125), (2 * q + 1, 0.75), (2 * q + 2, 0.375))


def transfer(taps, outs, out_pos, in_pos, n_out, n_in, scale):
    m = np.zeros((n_out, n_in), np.float32)
    for o in outs:
        for s, w in taps(o):
            row, col = out_pos(o), in_pos(scale * o + s if scale else s)
            if col is not None and 0 <= col < n_in:
                m[row, col] += w
    return m


def zdot(v, w):
    hi = v.astype(BF16)
    lo = (v - hi.astype(F32)).astype(BF16)
    return jnp.dot(hi, w, preferred_element_type=F32) + jnp.dot(
        lo, w, preferred_element_type=F32
    )


def exact(a, b):
    return jnp.dot(a, b, preferred_element_type=F32, precision=lax.Precision.HIGHEST)


def y_filters(mz, kz):
    rows = mz.shape[0]
    even = lax.broadcasted_iota(jnp.int32, mz.shape, 0) % 2 == 0

    def sums(v):
        s1 = pltpu.roll(v, 1, 0) + pltpu.roll(v, rows - 1, 0)
        s2 = pltpu.roll(v, 2, 0) + pltpu.roll(v, rows - 2, 0)
        return s1, jnp.where(even, s2, 0.0)

    m1, m2 = sums(mz)
    k1, k2 = sums(kz)
    md = jnp.where(even, 8.0, 16.0)
    kd = jnp.where(even, 14.0, 16.0)
    first = md * mz + 2.0 * m1 - m2
    second = (kd * mz - 8.0 * m1 + m2) + (md * kz + 2.0 * k1 - k2)
    return first, second


def kernel(
    geo, u_ref, b_ref, w0, w1, w2, rz0, ry0, rz1, ry1, pz1, py1, pz0, py0, out_ref,
    ue, be, d0, r0, a0, c0, packs, unpacks, blk, zin, g1, d1, r1, s1, a1, c1,
    r2, d2, a2, t2, send, recv, zsend, zrecv, gsend, grecv, gzsend, gzrecv,
):
    nx, ny, nz, bx, by, bz, wx, wy = geo
    ix, iy, iz = lax.axis_index("gx"), lax.axis_index("gy"), lax.axis_index("gz")
    full_x, full_y = wx == nx, wy == ny
    cx, cy, cz = bx // 2, by // 2, bz // 2
    start_x = 0 if full_x else ix - REACH
    start_y = 0 if full_y else iy - REACH

    def at(axis, off):
        return (
            ix + off if axis == 0 else ix,
            iy + off if axis == 1 else iy,
            iz + off if axis == 2 else iz,
        )

    place = (ix, iy, iz)
    counts = (nx, ny, nz)

    def there(axis, off):
        pos = place[axis] + off
        return (pos >= 0) & (pos < counts[axis])

    spans = (wx - 1 if full_x else REACH, wy - 1 if full_y else REACH, 1 if nz > 1 else 0)
    offsets = [[o for o in range(-s, s + 1) if o] for s in spans]

    ue[...] = jnp.zeros_like(ue)
    be[...] = jnp.zeros_like(be)
    unpacks[...] = jnp.zeros_like(unpacks)
    zin[...] = jnp.zeros_like(zin)
    g1[...] = jnp.zeros_like(g1)
    ue[H : H + bx, H : H + by, :bz] = u_ref[...]
    be[H : H + bx, H : H + by, :bz] = b_ref[...]

    barrier = pltpu.get_barrier_semaphore()
    total = 0
    for axis in range(3):
        for off in offsets[axis]:
            ok = there(axis, off)
            total = total + ok.astype(jnp.int32)

            @pl.when(ok)
            def _():
                pl.semaphore_signal(
                    barrier, inc=1, device_id=at(axis, off), device_id_type=MESH
                )

    pl.semaphore_wait(barrier, total)

    def remote(src, dst, ss, rs, axis, off):
        return pltpu.make_async_remote_copy(
            src_ref=src, dst_ref=dst, send_sem=ss, recv_sem=rs,
            device_id=at(axis, off), device_id_type=MESH,
        )

    def start_if(axis, off, copies):
        @pl.when(there(axis, off))
        def _():
            for c in copies:
                c.start()

    def recv_if(axis, off, copies):
        @pl.when(there(axis, -off))
        def _():
            for c in copies:
                c.wait_recv()

    def sent_if(axis, off, copies):
        @pl.when(there(axis, off))
        def _():
            for c in copies:
                c.wait_send()

    L = bz

    def x_copies(off):
        res = []
        for n, (ref, ext, w) in enumerate(((u_ref, ue, H), (b_ref, be, H - 2))):
            k = n * 2 + (off > 0)
            lo = bx - w if off > 0 else 0
            dst = H - w if off > 0 else H + bx
            res.append(
                remote(
                    ref.at[lo : lo + w],
                    ext.at[dst : dst + w, H : H + by, :L],
                    send.at[k], recv.at[k], 0, off,
                )
            )
        return res

    def y_copies(off):
        res = []
        for n, (ref, ext) in enumerate(((u_ref, ue), (b_ref, be))):
            k = 4 + n * 2 + (off > 0)
            lo = by - H if off > 0 else 0
            dst = 0 if off > 0 else H + by
            res.append(
                remote(
                    ref.at[:, lo : lo + H],
                    ext.at[H : H + bx, dst : dst + H, :L],
                    send.at[k], recv.at[k], 1, off,
                )
            )
        return res

    def corner_copies(off):
        res = []
        for n, (ext, w) in enumerate(((ue, H), (be, H - 2))):
            for side in range(2):
                k = 8 + n * 4 + side * 2 + (off > 0)
                xs = H - w if side == 0 else H + bx
                lo = by if off > 0 else H
                dst = 0 if off > 0 else H + by
                res.append(
                    remote(
                        ext.at[xs : xs + w, lo : lo + H, :L],
                        ext.at[xs : xs + w, dst : dst + H, :L],
                        send.at[k], recv.at[k], 1, off,
                    )
                )
        return res

    both = (-1, 1)
    for off in both:
        start_if(0, off, x_copies(off))
    for off in both:
        start_if(1, off, y_copies(off))
    for off in both:
        recv_if(0, off, x_copies(off))
    for off in both:
        start_if(1, off, corner_copies(off))
    for off in both:
        recv_if(1, off, y_copies(off) + corner_copies(off))

    per = L // H
    lane = lax.broadcasted_iota(jnp.int32, (by + 2 * H, L), 1)
    groups = (bx + 2 * H) // per
    if nz > 1:
        for n, ext in enumerate((ue, be)):
            for g in range(groups):
                low = jnp.zeros((by + 2 * H, L), F32)
                high = jnp.zeros((by + 2 * H, L), F32)
                for k in range(per):
                    plane = ext[g * per + k, :, :L]
                    here = (lane // H) == k
                    low = jnp.where(here, pltpu.roll(plane, (k * H) % L, 1), low)
                    high = jnp.where(here, pltpu.roll(plane, ((k + 1) * H) % L, 1), high)
                packs[0, n, g] = low
                packs[1, n, g] = high

        def z_copies(off):
            k = int(off > 0)
            return [remote(packs.at[k], unpacks.at[k], zsend.at[k], zrecv.at[k], 2, off)]

        for off in both:
            start_if(2, off, z_copies(off))
        for off in both:
            recv_if(2, off, z_copies(off))
        for n, ext in enumerate((ue, be)):
            for g in range(groups):
                upper, lower = unpacks[0, n, g], unpacks[1, n, g]
                for k in range(per):
                    up = pltpu.roll(upper, (L - k * H) % L, 1)
                    lo = pltpu.roll(lower, (L - (k + 1) * H) % L, 1)
                    ext[g * per + k, :, L:] = jnp.where(
                        lane < H, up, jnp.where(lane >= L - H, lo, 0.0)
                    )

    def masks_and_diagonals(level, rows, lanes, y_first, y_end, z_of_lane, z_ok, z_first):
        yy = lax.broadcasted_iota(jnp.int32, (rows, lanes), 0)
        zz = lax.broadcasted_iota(jnp.int32, (rows, lanes), 1)
        y_even, z_even = yy % 2 == 0, zz % 2 == 0
        gy = y_first + yy
        gz = z_first + z_of_lane(zz)
        n_y, n_z = (ny * by) >> level, (nz * bz) >> level
        ok = (gy >= 0) & (gy < n_y) & (yy < y_end) & (gz >= 0) & (gz < n_z) & z_ok(zz)
        mask = jnp.where(ok, 1.0, 0.0)
        my = jnp.where(y_even, 8.0, 16.0) / 30.0
        mz = jnp.where(z_even, 8.0, 16.0) / 30.0
        ky = jnp.where(y_even, 14.0, 16.0) / 3.0
        kz = jnp.where(z_even, 14.0, 16.0) / 3.0
        inv = []
        for kx, mx in ((14.0 / 3.0, 8.0 / 30.0), (16.0 / 3.0, 16.0 / 30.0)):
            diag = 2.0**level * (kx * my * mz + mx * ky * mz + mx * my * kz)
            inv.append(mask / diag)
        return mask, inv

    def filter_planes(src, w, acc, first, pairs, rows, lanes):
        def body(p, carry):
            x = first + 2 * p
            v = src[pl.ds(x, 2)].reshape(2 * rows, lanes)
            prod = zdot(v, w[...])
            for k in range(2):
                part = prod[k * rows : (k + 1) * rows]
                a, c = y_filters(part[:, :lanes], part[:, lanes:])
                acc[0, x + k] = a
                acc[1, x + k] = c
            return carry

        lax.fori_loop(0, pairs, body, 0)

    def applied(acc, first, pairs, level, use):
        scale = 2.0**level / 2700.0

        def body(p, carry):
            x = first + 2 * p
            a = [acc[0, x + k] for k in range(-2, 4)]
            c = [acc[1, x + k] for k in range(-2, 4)]
            even = (14.0 * a[2] - 8.0 * (a[1] + a[3]) + (a[0] + a[4])) + (
                8.0 * c[2] + 2.0 * (c[1] + c[3]) - (c[0] + c[4])
            )
            odd = (16.0 * a[3] - 8.0 * (a[2] + a[4])) + (16.0 * c[3] + 2.0 * (c[2] + c[4]))
            use(x, 0, scale * even)
            use(x + 1, 1, scale * odd)
            return carry

        lax.fori_loop(0, pairs, body, 0)

    rows0, lanes0 = by + 2 * H, 2 * bz
    mask0, inv0 = masks_and_diagonals(
        0, rows0, lanes0, iy * by - H, rows0,
        lambda z: jnp.where(z < bz + bz // 2, z, z - 2 * bz), lambda z: z >= 0, iz * bz,
    )

    def x_mask(level, x, x_first):
        g = x_first + x
        return jnp.where((g >= 0) & (g < ((nx * bx) >> level)), 1.0, 0.0).astype(F32)

    gx0 = ix * bx - H

    def use_residual(x, odd, av):
        r = be[x] - av
        r0[x] = r
        d0[x] = (inv0[odd] * (FIRST * x_mask(0, x, gx0))) * r

    filter_planes(ue, w0, a0, 0, (bx + 16) // 2, rows0, lanes0)
    applied(a0, 2, (bx + 12) // 2, 0, use_residual)
    own0 = (slice(H, H + bx), slice(H, H + by), slice(0, bz))
    out_ref[...] = u_ref[...] + d0[own0]

    def use_step(x, odd, av):
        r = r0[x] - av
        r0[x] = r
        d0[x] = KEEP * d0[x] + (inv0[odd] * (STEP * x_mask(0, x, gx0))) * r

    filter_planes(d0, w0, a0, 2, (bx + 12) // 2, rows0, lanes0)
    applied(a0, 4, (bx + 8) // 2, 0, use_step)
    out_ref[...] += d0[own0]

    def use_down(x, odd, av):
        r0[x] = (r0[x] - av) * (mask0 * x_mask(0, x, gx0))

    filter_planes(d0, w0, a0, 2, (bx + 10) // 2, rows0, lanes0)
    applied(a0, 4, (bx + 6) // 2, 0, use_down)

    def narrowed(ref, x):
        even = (
            ref[x] + 0.375 * (ref[x - 1] + ref[x + 1]) - 0.125 * (ref[x - 3] + ref[x + 3])
        )
        odd = ref[x + 2] + 0.75 * (ref[x + 1] + ref[x + 3])
        return even, odd

    coarse = []
    for q in range(cx // 2):
        for plane in narrowed(r0, H + 4 * q):
            coarse.append(exact(ry0[...], plane))
    rhs = zdot(jnp.concatenate(coarse, axis=0), rz0[...])
    wl = cz + 2 * ZR
    blk[...] = rhs.reshape(cx, cy, wl)

    if nz > 1:

        def gz_copies(off):
            k = int(off > 0)
            return [remote(blk, zin.at[k], gzsend.at[k], gzrecv.at[k], 2, off)]

        for off in both:
            start_if(2, off, gz_copies(off))
        for off in both:
            recv_if(2, off, gz_copies(off))
        wlane = lax.broadcasted_iota(jnp.int32, (cy, wl), 1)
        for p in range(cx):
            lower = pltpu.roll(zin[1, p], wl - cz, 1)
            upper = pltpu.roll(zin[0, p], cz, 1)
            zin[2, p] = jnp.where(
                wlane < ZR, lower, jnp.where(wlane >= ZR + cz, upper, blk[p])
            )
    else:
        zin[2] = blk[...]

    def slot(axis, off):
        if (full_x, full_y)[axis]:
            return (ix, iy)[axis]
        return REACH - off

    def spot(axis, off, size):
        return pl.ds(pl.multiple_of(slot(axis, off) * size, size), size)

    def gx_copies(off):
        k = off + REACH * 2
        dst = g1.at[spot(0, off, cx), spot(1, 0, cy)]
        return [remote(zin.at[2], dst, gsend.at[0, k], grecv.at[0, k], 0, off)]

    def gy_copies(off):
        k = off + REACH * 2
        src = g1.at[:, spot(1, 0, cy)]
        dst = g1.at[:, spot(1, off, cy)]
        return [remote(src, dst, gsend.at[1, k], grecv.at[1, k], 1, off)]

    for off in offsets[0]:
        start_if(0, off, gx_copies(off))
    g1[spot(0, 0, cx), spot(1, 0, cy)] = zin[2]
    rows1, planes1 = cy * wy + 8, cx * wx
    d1[...] = jnp.zeros_like(d1)
    a1[...] = jnp.zeros_like(a1)
    d2[...] = jnp.zeros_like(d2)
    a2[...] = jnp.zeros_like(a2)
    c1[...] = jnp.zeros_like(c1)
    r1[...] = jnp.zeros_like(r1)
    t2[...] = jnp.zeros_like(t2)
    for off in offsets[0]:
        recv_if(0, off, gx_copies(off))
    for off in offsets[1]:
        start_if(1, off, gy_copies(off))
    for off in offsets[1]:
        recv_if(1, off, gy_copies(off))

    Q = 8
    mask1, inv1 = masks_and_diagonals(
        1, rows1, wl, start_y * cy, cy * wy, lambda z: z, lambda z: z >= 0, iz * cz - ZR
    )
    gx1 = start_x * cx - Q

    def first_mid(p, carry):
        for odd in range(2):
            x = 2 * p + odd
            r = g1[x]
            r1[x + Q] = r
            d = (inv1[odd] * (FIRST * x_mask(1, x + Q, gx1))) * r
            d1[x + Q] = d
            s1[x] = d
        return carry

    lax.fori_loop(0, planes1 // 2, first_mid, 0)

    def use_step1(x, odd, av):
        r = r1[x] - av
        r1[x] = r
        d = KEEP * d1[x] + (inv1[odd] * (STEP * x_mask(1, x, gx1))) * r
        d1[x] = d
        s1[x - Q] += d

    def use_down1(x, odd, av):
        r1[x] = (r1[x] - av) * (mask1 * x_mask(1, x, gx1))

    half1 = planes1 // 2
    filter_planes(d1, w1, a1, Q, half1, rows1, wl)
    applied(a1, Q, half1, 1, use_step1)
    filter_planes(d1, w1, a1, Q, half1, rows1, wl)
    applied(a1, Q, half1, 1, use_down1)

    planes2 = planes1 // 2
    rows2 = cy * wy // 2 + 8
    mask2, inv2 = masks_and_diagonals(
        2, rows2, wl, start_y * (cy // 2), cy * wy // 2, lambda z: z,
        lambda z: z < wl // 2, iz * (cz // 2) - ZR // 2,
    )
    gx2 = start_x * (cx // 2) - Q

    def down_mid(q, carry):
        parts = [exact(ry1[...], plane) for plane in narrowed(r1, Q + 4 * q)]
        prod = zdot(jnp.concatenate(parts, axis=0), rz1[...])
        for odd in range(2):
            x = 2 * q + odd + Q
            r = prod[odd * rows2 : (odd + 1) * rows2]
            r2[x] = r
            d2[x] = (inv2[odd] * (FIRST * x_mask(2, x, gx2))) * r
        return carry

    lax.fori_loop(0, planes2 // 2, down_mid, 0)
    filter_planes(d2, w2, a2, Q, planes2 // 2, rows2, wl)

    def use_last(x, odd, av):
        r = r2[x] - av
        d2[x] = (1.0 + KEEP) * d2[x] + (inv2[odd] * (STEP * x_mask(2, x, gx2))) * r

    applied(a2, Q, planes2 // 2, 2, use_last)

    def up_last(p, carry):
        v = zdot(d2[pl.ds(Q + 2 * p, 2)].reshape(2 * rows2, wl), pz1[...])
        for k in range(2):
            t2[2 * p + k] = exact(py1[...], v[k * rows2 : (k + 1) * rows2])
        return carry

    lax.fori_loop(0, planes2 // 2, up_last, 0)

    def widened(ref, x):
        one, two, three = ref[x], ref[x + 1], ref[x + 2]
        return (
            one,
            0.375 * one + 0.75 * two - 0.125 * three,
            two,
            -0.125 * one + 0.75 * two + 0.375 * three,
        )

    def up_mid(q, carry):
        for k, plane in enumerate(widened(t2, 2 * q)):
            x = 4 * q + k
            e = plane * (mask1 * x_mask(1, x + Q, gx1))
            d1[x + Q] = e
            s1[x] += e
        return carry

    lax.fori_loop(0, planes1 // 4, up_mid, 0)
    filter_planes(d1, w1, a1, Q, half1, rows1, wl)

    def use_up1(x, odd, av):
        r = r1[x] - av
        r1[x] = r
        d = (inv1[odd] * (FIRST * x_mask(1, x, gx1))) * r
        d1[x] = d
        s1[x - Q] += d

    applied(a1, Q, half1, 1, use_up1)
    filter_planes(d1, w1, a1, Q, half1, rows1, wl)

    def use_final1(x, odd, av):
        r = r1[x] - av
        d = KEEP * d1[x] + (inv1[odd] * (STEP * x_mask(1, x, gx1))) * r
        c1[x, 8 : 8 + rows1] = s1[x - Q] + d

    applied(a1, Q, half1, 1, use_final1)

    crow = cy + 16
    own_x = (ix if full_x else REACH) * cx + Q
    own_y = pl.multiple_of((iy if full_y else REACH) * cy, 8)

    def up_first(p, carry):
        x = own_x - 2 + 2 * p
        v = c1[pl.ds(x, 2), pl.ds(own_y, crow)].reshape(2 * crow, wl)
        v = zdot(v, pz0[...])
        for k in range(2):
            c0[2 * p + k] = exact(py0[...], v[k * crow : (k + 1) * crow])
        return carry

    lax.fori_loop(0, (cx + 6) // 2, up_first, 0)

    def up_fine(q, carry):
        for k, plane in enumerate(widened(c0, 2 * q)):
            x = H - 4 + 4 * q + k
            d0[x] = plane * (mask0 * x_mask(0, x, gx0))
        return carry

    lax.fori_loop(0, (bx + 8) // 4, up_fine, 0)
    out_ref[...] += d0[own0]
    filter_planes(d0, w0, a0, 4, (bx + 8) // 2, rows0, lanes0)

    def use_up(x, odd, av):
        r = r0[x] - av
        r0[x] = r
        d0[x] = (inv0[odd] * (FIRST * x_mask(0, x, gx0))) * r

    applied(a0, 6, (bx + 4) // 2, 0, use_up)
    filter_planes(d0, w0, a0, 6, (bx + 4) // 2, rows0, lanes0)

    def use_final(x, odd, av):
        r = r0[x] - av
        d = d0[x]
        new = d + (KEEP * d + (inv0[odd] * STEP) * r)
        out_ref[x - H] += new[H : H + by, :bz]

    applied(a0, H, bx // 2, 0, use_final)

    for off in both:
        sent_if(0, off, x_copies(off))
        sent_if(1, off, y_copies(off) + corner_copies(off))
        if nz > 1:
            sent_if(2, off, z_copies(off) + gz_copies(off))
    for off in offsets[0]:
        sent_if(0, off, gx_copies(off))
    for off in offsets[1]:
        sent_if(1, off, gy_copies(off))


def local(mesh_shape, u, b):
    nx, ny, nz = (mesh_shape[a] for a in ("gx", "gy", "gz"))
    bx, by, bz = u.shape
    cx, cy, cz = bx // 2, by // 2, bz // 2
    wx = nx if nx <= 2 * REACH + 1 else 2 * REACH + 1
    wy = ny if ny <= 2 * REACH + 1 else 2 * REACH + 1
    wl = cz + 2 * ZR
    rows0, lanes0 = by + 2 * H, 2 * bz
    rows1, planes1 = cy * wy + 8, cx * wx
    rows2, planes2 = cy * wy // 2 + 8, planes1 // 2
    crow = cy + 16

    def z_pos(z):
        return z if z >= 0 else z + lanes0

    w0 = band_matrices(lanes0, True)
    w1 = band_matrices(wl, False)
    w2 = band_matrices(wl, False)
    rz0 = transfer(restrict_taps, range(cz), lambda o: o + ZR, z_pos, wl, lanes0, 2).T
    ry0 = transfer(restrict_taps, range(cy), lambda o: o, lambda f: f + H, cy, rows0, 2)
    rz1 = transfer(restrict_taps, range(wl // 2), lambda o: o, lambda f: f, wl, wl, 2).T
    live1 = lambda f: f if 0 <= f < cy * wy else None
    ry1 = transfer(restrict_taps, range(cy * wy // 2), lambda o: o, live1, rows2, rows1, 2)
    pz1 = transfer(prolong_taps, range(wl), lambda o: o, lambda c: c, wl, wl, 0).T
    live2 = lambda c: c if 0 <= c < cy * wy // 2 else None
    py1 = transfer(prolong_taps, range(cy * wy), lambda o: o, live2, rows1, rows2, 0)
    pz0 = transfer(
        prolong_taps, range(-H, bz + H), z_pos, lambda c: c + ZR, lanes0, wl, 0
    ).T
    py0 = transfer(
        prolong_taps, range(-H, by + H), lambda o: o + H, lambda c: c + 8, rows0, crow, 0
    )
    bf = lambda m: jnp.asarray(m, BF16)
    fl = lambda m: jnp.asarray(m, F32)
    consts = (
        bf(w0), bf(w1), bf(w2), bf(rz0), fl(ry0), bf(rz1), fl(ry1), bf(pz1), fl(py1),
        bf(pz0), fl(py0),
    )
    vm = lambda *s: pltpu.VMEM(s, F32)
    groups = (bx + 2 * H) // (bz // H)
    dma = lambda *s: pltpu.SemaphoreType.DMA(s)
    geo = (nx, ny, nz, bx, by, bz, wx, wy)
    return pl.pallas_call(
        functools.partial(kernel, geo),
        out_shape=jax.ShapeDtypeStruct(u.shape, F32),
        in_specs=[pl.BlockSpec(memory_space=pltpu.VMEM)] * (2 + len(consts)),
        out_specs=pl.BlockSpec(memory_space=pltpu.VMEM),
        scratch_shapes=[
            vm(bx + 16, rows0, lanes0), vm(bx + 16, rows0, lanes0),
            vm(bx + 16, rows0, lanes0), vm(bx + 16, rows0, lanes0),
            vm(2, bx + 16, rows0, lanes0), vm(cx + 8, rows0, lanes0),
            vm(2, 2, groups, rows0, bz), vm(2, 2, groups, rows0, bz),
            vm(cx, cy, wl), vm(3, cx, cy, wl),
            vm(planes1, rows1, wl), vm(planes1 + 16, rows1, wl),
            vm(planes1 + 16, rows1, wl), vm(planes1, rows1, wl),
            vm(2, planes1 + 16, rows1, wl), vm(planes1 + 16, rows1 + 8, wl),
            vm(planes2 + 16, rows2, wl), vm(planes2 + 16, rows2, wl),
            vm(2, planes2 + 16, rows2, wl), vm(planes2 + 8, rows1, wl),
            dma(16), dma(16), dma(2), dma(2),
            dma(2, 4 * REACH + 1), dma(2, 4 * REACH + 1), dma(2), dma(2),
        ],
        compiler_params=pltpu.CompilerParams(
            collective_id=0, has_side_effects=True, vmem_limit_bytes=60 * 1024 * 1024
        ),
    )(u, b, *consts)


def solution(mesh):
    placed = P("gx", "gy", "gz")
    return jax.shard_map(
        functools.partial(local, dict(mesh.shape)), mesh=mesh,
        in_specs=(placed, placed), out_specs=placed, check_vma=False,
    )
```

time: 276 us -> 77.3 us (0.28)
  starting transfers between devices: 147 us -> 0 us
  waiting for transfers between devices: 108 us -> 0 us
  Pallas kernels: 0 us -> 75.6 us
  other arithmetic: 11.2 us -> 0 us
  matrix products: 3.92 us -> 0 us
    ppermute x60 -> x0, starting transfers between devices: 147 us -> none  [the longest x27 92.1 us: extended_2(): before = lax.ppermute(last, axis, up)]
    ppermute x60 -> x0, waiting for transfers between devices: 108 us -> none  [the longest x27 82.8 us: extended_2(): after = lax.ppermute(leading, axis, down)]
    pallas_call x0 -> x1, Pallas kernels: none -> 75.6 us  [local(): pl.pallas_call(functools.partial(kernel, geo), out_shape=jax.ShapeDtypeSt...]
    add x31 -> x0, other arithmetic: 6.85 us -> none  [the longest x26 5.3 us: along_axis(): summed = weight * shifted if offset == 0 else summed + weight * shifted]
    dot_general x12 -> x0, matrix products: 3.92 us -> none  [along_dim_product(): jnp.einsum(einsum_forms[dim_index], matrix, values, precision=lax.Precisi...]
  transfers between devices with their start and end apart: 60 -> 0, of which waited for: 42 -> 0; matrix products, arithmetic and copies ran while one was open for 0% -> 0% of each run, Pallas kernels for 0% -> 0%
where the time goes in v1:
time: 77.3 us; the launch traced here: 77.2 us
  Pallas kernels  75.6 us (98%)
  local copies, waits for them, and re-layouts  1.57 us (2%)
    pallas_call x1, Pallas kernels, local(): pl.pallas_call(functools.partial(kernel, geo), out_shape=jax.ShapeDtypeSt...  75.6 us
    unnamed x1, local copies, waits for them, and re-layouts  1.57 us

profile of v1, /device:TPU:1, one launch (start us, length us, event | category | flops | bytes accessed | tf_op | source)
XLA Modules:
  0.0 77.2 jit_solution(5826699574709321972)
XLA Ops:
  0.0 75.6 %shard_map.127 = f32[16,16,128]{2,1,0:T(8,128)} custom-call(f32[16,16,128]{2,1,0:T(8,128)} %u_ref.1, f32[16,16,128]{2,1,0:T(8,128)} %b_ref.1, bf16[256,512]{1,0:T(8,128)(2,1)} %constant.20.clone.w0, bf16[128,256]{1,0:T(8,128)(2,1)} %constant.21.clone.w1.w2, bf16[128,256]{1,0:T(8,128)(2,1)} %constant.21.clone.w1.w2, bf16[256,128]{1,0:T(8,128)(2,1)} %constant.22.clone.rz0, ...), custom_call_target="tpu_custom_call" | custom-call | tf_op jit(solution)/shard_map/pallas_call | solution.py:627
  75.6 1.6 %copy.15 = f32[16,16,128]{2,1,0:T(8,128)} copy(f32[16,16,128]{2,1,0:T(8,128)} %shard_map.127) | data formatting | bytes 262144

commit v2 on v1

--- a/solution.py
+++ b/solution.py
@@ -20,24 +20,6 @@
 FIRST = 1.0 / 1.32
 KEEP = RHO1 * RHO0
 STEP = 2.0 * RHO1 / 1.1
-
-
-def band_matrices(size, cyclic):
-    mass = np.zeros((size, size), np.float32)
-    stiff = np.zeros((size, size), np.float32)
-    for out in range(size):
-        if out % 2 == 0:
-            taps = ((-2, -1, 1), (-1, 2, -8), (0, 8, 14), (1, 2, -8), (2, -1, 1))
-        else:
-            taps = ((-1, 2, -8), (0, 16, 16), (1, 2, -8))
-        for off, m, k in taps:
-            src = out + off
-            if cyclic:
-                src %= size
-            if 0 <= src < size:
-                mass[src, out] += m
-                stiff[src, out] += k
-    return np.concatenate([mass, stiff], axis=1)
 
 
 def restrict_taps(g):
@@ -77,6 +59,16 @@
     return jnp.dot(a, b, preferred_element_type=F32, precision=lax.Precision.HIGHEST)
 
 
+def z_filters(v):
+    lanes = v.shape[1]
+    even = lax.broadcasted_iota(jnp.int32, v.shape, 1) % 2 == 0
+    s1 = pltpu.roll(v, 1, 1) + pltpu.roll(v, lanes - 1, 1)
+    s2 = jnp.where(even, pltpu.roll(v, 2, 1) + pltpu.roll(v, lanes - 2, 1), 0.0)
+    md = jnp.where(even, 8.0, 16.0)
+    kd = jnp.where(even, 14.0, 16.0)
+    return md * v + 2.0 * s1 - s2, kd * v - 8.0 * s1 + s2
+
+
 def y_filters(mz, kz):
     rows = mz.shape[0]
     even = lax.broadcasted_iota(jnp.int32, mz.shape, 0) % 2 == 0
@@ -96,7 +88,7 @@
 
 
 def kernel(
-    geo, u_ref, b_ref, w0, w1, w2, rz0, ry0, rz1, ry1, pz1, py1, pz0, py0, out_ref,
+    geo, u_ref, b_ref, rz0, ry0, rz1, ry1, pz1, py1, pz0, py0, out_ref,
     ue, be, d0, r0, a0, c0, packs, unpacks, blk, zin, g1, d1, r1, s1, a1, c1,
     r2, d2, a2, t2, send, recv, zsend, zrecv, gsend, grecv, gzsend, gzrecv,
 ):
@@ -285,14 +277,11 @@
             inv.append(mask / diag)
         return mask, inv
 
-    def filter_planes(src, w, acc, first, pairs, rows, lanes):
+    def filter_planes(src, acc, first, pairs):
         def body(p, carry):
             x = first + 2 * p
-            v = src[pl.ds(x, 2)].reshape(2 * rows, lanes)
-            prod = zdot(v, w[...])
             for k in range(2):
-                part = prod[k * rows : (k + 1) * rows]
-                a, c = y_filters(part[:, :lanes], part[:, lanes:])
+                a, c = y_filters(*z_filters(src[x + k]))
                 acc[0, x + k] = a
                 acc[1, x + k] = c
             return carry
@@ -304,14 +293,18 @@
 
         def body(p, carry):
             x = first + 2 * p
-            a = [acc[0, x + k] for k in range(-2, 4)]
-            c = [acc[1, x + k] for k in range(-2, 4)]
-            even = (14.0 * a[2] - 8.0 * (a[1] + a[3]) + (a[0] + a[4])) + (
-                8.0 * c[2] + 2.0 * (c[1] + c[3]) - (c[0] + c[4])
-            )
-            odd = (16.0 * a[3] - 8.0 * (a[2] + a[4])) + (16.0 * c[3] + 2.0 * (c[2] + c[4]))
-            use(x, 0, scale * even)
-            use(x + 1, 1, scale * odd)
+            for t in range(acc.shape[2] // 8):
+                y = slice(8 * t, 8 * t + 8)
+                a = [acc[0, x + k, y] for k in range(-2, 4)]
+                c = [acc[1, x + k, y] for k in range(-2, 4)]
+                even = (14.0 * a[2] - 8.0 * (a[1] + a[3]) + (a[0] + a[4])) + (
+                    8.0 * c[2] + 2.0 * (c[1] + c[3]) - (c[0] + c[4])
+                )
+                odd = (16.0 * a[3] - 8.0 * (a[2] + a[4])) + (
+                    16.0 * c[3] + 2.0 * (c[2] + c[4])
+                )
+                use(x, 0, scale * even, t)
+                use(x + 1, 1, scale * odd, t)
             return carry
 
         lax.fori_loop(0, pairs, body, 0)
@@ -328,29 +321,35 @@
 
     gx0 = ix * bx - H
 
-    def use_residual(x, odd, av):
-        r = be[x] - av
-        r0[x] = r
-        d0[x] = (inv0[odd] * (FIRST * x_mask(0, x, gx0))) * r
-
-    filter_planes(ue, w0, a0, 0, (bx + 16) // 2, rows0, lanes0)
+    def tile(t):
+        return slice(8 * t, 8 * t + 8)
+
+    def use_residual(x, odd, av, t):
+        y = tile(t)
+        r = be[x, y] - av
+        r0[x, y] = r
+        d0[x, y] = (inv0[odd][y] * (FIRST * x_mask(0, x, gx0))) * r
+
+    filter_planes(ue, a0, 0, (bx + 16) // 2)
     applied(a0, 2, (bx + 12) // 2, 0, use_residual)
     own0 = (slice(H, H + bx), slice(H, H + by), slice(0, bz))
     out_ref[...] = u_ref[...] + d0[own0]
 
-    def use_step(x, odd, av):
-        r = r0[x] - av
-        r0[x] = r
-        d0[x] = KEEP * d0[x] + (inv0[odd] * (STEP * x_mask(0, x, gx0))) * r
-
-    filter_planes(d0, w0, a0, 2, (bx + 12) // 2, rows0, lanes0)
+    def use_step(x, odd, av, t):
+        y = tile(t)
+        r = r0[x, y] - av
+        r0[x, y] = r
+        d0[x, y] = KEEP * d0[x, y] + (inv0[odd][y] * (STEP * x_mask(0, x, gx0))) * r
+
+    filter_planes(d0, a0, 2, (bx + 12) // 2)
     applied(a0, 4, (bx + 8) // 2, 0, use_step)
     out_ref[...] += d0[own0]
 
-    def use_down(x, odd, av):
-        r0[x] = (r0[x] - av) * (mask0 * x_mask(0, x, gx0))
-
-    filter_planes(d0, w0, a0, 2, (bx + 10) // 2, rows0, lanes0)
+    def use_down(x, odd, av, t):
+        y = tile(t)
+        r0[x, y] = (r0[x, y] - av) * (mask0[y] * x_mask(0, x, gx0))
+
+    filter_planes(d0, a0, 2, (bx + 10) // 2)
     applied(a0, 4, (bx + 6) // 2, 0, use_down)
 
     def narrowed(ref, x):
@@ -443,20 +442,22 @@
 
     lax.fori_loop(0, planes1 // 2, first_mid, 0)
 
-    def use_step1(x, odd, av):
-        r = r1[x] - av
-        r1[x] = r
-        d = KEEP * d1[x] + (inv1[odd] * (STEP * x_mask(1, x, gx1))) * r
-        d1[x] = d
-        s1[x - Q] += d
-
-    def use_down1(x, odd, av):
-        r1[x] = (r1[x] - av) * (mask1 * x_mask(1, x, gx1))
+    def use_step1(x, odd, av, t):
+        y = tile(t)
+        r = r1[x, y] - av
+        r1[x, y] = r
+        d = KEEP * d1[x, y] + (inv1[odd][y] * (STEP * x_mask(1, x, gx1))) * r
+        d1[x, y] = d
+        s1[x - Q, y] += d
+
+    def use_down1(x, odd, av, t):
+        y = tile(t)
+        r1[x, y] = (r1[x, y] - av) * (mask1[y] * x_mask(1, x, gx1))
 
     half1 = planes1 // 2
-    filter_planes(d1, w1, a1, Q, half1, rows1, wl)
+    filter_planes(d1, a1, Q, half1)
     applied(a1, Q, half1, 1, use_step1)
-    filter_planes(d1, w1, a1, Q, half1, rows1, wl)
+    filter_planes(d1, a1, Q, half1)
     applied(a1, Q, half1, 1, use_down1)
 
     planes2 = planes1 // 2
@@ -478,11 +479,13 @@
         return carry
 
     lax.fori_loop(0, planes2 // 2, down_mid, 0)
-    filter_planes(d2, w2, a2, Q, planes2 // 2, rows2, wl)
-
-    def use_last(x, odd, av):
-        r = r2[x] - av
-        d2[x] = (1.0 + KEEP) * d2[x] + (inv2[odd] * (STEP * x_mask(2, x, gx2))) * r
+    filter_planes(d2, a2, Q, planes2 // 2)
+
+    def use_last(x, odd, av, t):
+        y = tile(t)
+        r = r2[x, y] - av
+        step = (inv2[odd][y] * (STEP * x_mask(2, x, gx2))) * r
+        d2[x, y] = (1.0 + KEEP) * d2[x, y] + step
 
     applied(a2, Q, planes2 // 2, 2, use_last)
 
@@ -512,22 +515,24 @@
         return carry
 
     lax.fori_loop(0, planes1 // 4, up_mid, 0)
-    filter_planes(d1, w1, a1, Q, half1, rows1, wl)
-
-    def use_up1(x, odd, av):
-        r = r1[x] - av
-        r1[x] = r
-        d = (inv1[odd] * (FIRST * x_mask(1, x, gx1))) * r
-        d1[x] = d
-        s1[x - Q] += d
+    filter_planes(d1, a1, Q, half1)
+
+    def use_up1(x, odd, av, t):
+        y = tile(t)
+        r = r1[x, y] - av
+        r1[x, y] = r
+        d = (inv1[odd][y] * (FIRST * x_mask(1, x, gx1))) * r
+        d1[x, y] = d
+        s1[x - Q, y] += d
 
     applied(a1, Q, half1, 1, use_up1)
-    filter_planes(d1, w1, a1, Q, half1, rows1, wl)
-
-    def use_final1(x, odd, av):
-        r = r1[x] - av
-        d = KEEP * d1[x] + (inv1[odd] * (STEP * x_mask(1, x, gx1))) * r
-        c1[x, 8 : 8 + rows1] = s1[x - Q] + d
+    filter_planes(d1, a1, Q, half1)
+
+    def use_final1(x, odd, av, t):
+        y = tile(t)
+        r = r1[x, y] - av
+        d = KEEP * d1[x, y] + (inv1[odd][y] * (STEP * x_mask(1, x, gx1))) * r
+        c1[x, tile(t + 1)] = s1[x - Q, y] + d
 
     applied(a1, Q, half1, 1, use_final1)
 
@@ -553,21 +558,25 @@
 
     lax.fori_loop(0, (bx + 8) // 4, up_fine, 0)
     out_ref[...] += d0[own0]
-    filter_planes(d0, w0, a0, 4, (bx + 8) // 2, rows0, lanes0)
-
-    def use_up(x, odd, av):
-        r = r0[x] - av
-        r0[x] = r
-        d0[x] = (inv0[odd] * (FIRST * x_mask(0, x, gx0))) * r
+    filter_planes(d0, a0, 4, (bx + 8) // 2)
+
+    def use_up(x, odd, av, t):
+        y = tile(t)
+        r = r0[x, y] - av
+        r0[x, y] = r
+        d0[x, y] = (inv0[odd][y] * (FIRST * x_mask(0, x, gx0))) * r
 
     applied(a0, 6, (bx + 4) // 2, 0, use_up)
-    filter_planes(d0, w0, a0, 6, (bx + 4) // 2, rows0, lanes0)
-
-    def use_final(x, odd, av):
-        r = r0[x] - av
-        d = d0[x]
-        new = d + (KEEP * d + (inv0[odd] * STEP) * r)
-        out_ref[x - H] += new[H : H + by, :bz]
+    filter_planes(d0, a0, 6, (bx + 4) // 2)
+
+    def use_final(x, odd, av, t):
+        if t == 0 or t == by // 8 + 1:
+            return
+        y = tile(t)
+        r = r0[x, y] - av
+        d = d0[x, y]
+        new = d + (KEEP * d + (inv0[odd][y] * STEP) * r)
+        out_ref[x - H, tile(t - 1)] += new[:, :bz]
 
     applied(a0, H, bx // 2, 0, use_final)
 
@@ -597,9 +606,6 @@
     def z_pos(z):
         return z if z >= 0 else z + lanes0
 
-    w0 = band_matrices(lanes0, True)
-    w1 = band_matrices(wl, False)
-    w2 = band_matrices(wl, False)
     rz0 = transfer(restrict_taps, range(cz), lambda o: o + ZR, z_pos, wl, lanes0, 2).T
     ry0 = transfer(restrict_taps, range(cy), lambda o: o, lambda f: f + H, cy, rows0, 2)
     rz1 = transfer(restrict_taps, range(wl // 2), lambda o: o, lambda f: f, wl, wl, 2).T
@@ -617,7 +623,7 @@
     bf = lambda m: jnp.asarray(m, BF16)
     fl = lambda m: jnp.asarray(m, F32)
     consts = (
-        bf(w0), bf(w1), bf(w2), bf(rz0), fl(ry0), bf(rz1), fl(ry1), bf(pz1), fl(py1),
+        bf(rz0), fl(ry0), bf(rz1), fl(ry1), bf(pz1), fl(py1),
         bf(pz0), fl(py0),
     )
     vm = lambda *s: pltpu.VMEM(s, F32)

time: 77.3 us -> 70 us (0.906)
  Pallas kernels: 75.6 us -> 68.3 us
    pallas_call x1, Pallas kernels: 75.6 us -> 68.3 us  [local(): pl.pallas_call(functools.partial(kernel, geo), out_shape=jax.ShapeDtypeSt...]
where the time goes in v2:
time: 70 us; the launch traced here: 69.8 us
  Pallas kernels  68.3 us (98%)
  local copies, waits for them, and re-layouts  1.57 us (2%)
    pallas_call x1, Pallas kernels, local(): pl.pallas_call(functools.partial(kernel, geo), out_shape=jax.ShapeDtypeSt...  68.3 us
    unnamed x1, local copies, waits for them, and re-layouts  1.57 us

profile of v2, /device:TPU:1, one launch (start us, length us, event | category | flops | bytes accessed | tf_op | source)
XLA Modules:
  0.0 69.8 jit_solution(6794605980776690318)
XLA Ops:
  0.0 68.3 %shard_map.100 = f32[16,16,128]{2,1,0:T(8,128)} custom-call(f32[16,16,128]{2,1,0:T(8,128)} %u_ref.1, f32[16,16,128]{2,1,0:T(8,128)} %b_ref.1, bf16[256,128]{1,0:T(8,128)(2,1)} %constant.16.clone.rz0, f32[8,32]{1,0:T(8,128)} %constant.17.clone.ry0, bf16[128,128]{1,0:T(8,128)(2,1)} %constant.18.clone.rz1, f32[24,40]{1,0:T(8,128)} %constant.19.clone.ry1, ...), custom_call_target="tpu_custom_call" | custom-call | tf_op jit(solution)/shard_map/pallas_call | solution.py:633
  68.3 1.6 %copy.12 = f32[16,16,128]{2,1,0:T(8,128)} copy(f32[16,16,128]{2,1,0:T(8,128)} %shard_map.100) | data formatting | bytes 262144

commit v3 on v2

--- a/solution.py
+++ b/solution.py
@@ -64,32 +64,14 @@
     even = lax.broadcasted_iota(jnp.int32, v.shape, 1) % 2 == 0
     s1 = pltpu.roll(v, 1, 1) + pltpu.roll(v, lanes - 1, 1)
     s2 = jnp.where(even, pltpu.roll(v, 2, 1) + pltpu.roll(v, lanes - 2, 1), 0.0)
-    md = jnp.where(even, 8.0, 16.0)
-    kd = jnp.where(even, 14.0, 16.0)
-    return md * v + 2.0 * s1 - s2, kd * v - 8.0 * s1 + s2
-
-
-def y_filters(mz, kz):
-    rows = mz.shape[0]
-    even = lax.broadcasted_iota(jnp.int32, mz.shape, 0) % 2 == 0
-
-    def sums(v):
-        s1 = pltpu.roll(v, 1, 0) + pltpu.roll(v, rows - 1, 0)
-        s2 = pltpu.roll(v, 2, 0) + pltpu.roll(v, rows - 2, 0)
-        return s1, jnp.where(even, s2, 0.0)
-
-    m1, m2 = sums(mz)
-    k1, k2 = sums(kz)
-    md = jnp.where(even, 8.0, 16.0)
-    kd = jnp.where(even, 14.0, 16.0)
-    first = md * mz + 2.0 * m1 - m2
-    second = (kd * mz - 8.0 * m1 + m2) + (md * kz + 2.0 * k1 - k2)
-    return first, second
+    m = jnp.where(even, 8.0, 16.0) * v + 2.0 * s1 - s2
+    w = jnp.where(even, -2.0, -16.0) * v - 12.0 * s1 + 3.0 * s2
+    return m, w
 
 
 def kernel(
     geo, u_ref, b_ref, rz0, ry0, rz1, ry1, pz1, py1, pz0, py0, out_ref,
-    ue, be, d0, r0, a0, c0, packs, unpacks, blk, zin, g1, d1, r1, s1, a1, c1,
+    ue, be, d0, r0, a0, c0, packs, unpacks, y0, y1, y2, blk, zin, g1, d1, r1, s1, a1, c1,
     r2, d2, a2, t2, send, recv, zsend, zrecv, gsend, grecv, gzsend, gzrecv,
 ):
     nx, ny, nz, bx, by, bz, wx, wy = geo
@@ -119,6 +101,7 @@
     ue[...] = jnp.zeros_like(ue)
     be[...] = jnp.zeros_like(be)
     unpacks[...] = jnp.zeros_like(unpacks)
+    y0[...] = jnp.zeros_like(y0)
     zin[...] = jnp.zeros_like(zin)
     g1[...] = jnp.zeros_like(g1)
     ue[H : H + bx, H : H + by, :bz] = u_ref[...]
@@ -277,34 +260,65 @@
             inv.append(mask / diag)
         return mask, inv
 
-    def filter_planes(src, acc, first, pairs):
+    def filter_planes(src, lines, acc, first, pairs):
+        rows, lanes = src.shape[1], src.shape[2]
+
+        def body(p, carry):
+            x = first + 4 * p
+            for k in range(4):
+                m, w = z_filters(src[x + k])
+                for lt in range(lanes // 128):
+                    cut = slice(128 * lt, 128 * lt + 128)
+                    lines[k, 0, lt, 8 : 8 + rows] = m[:, cut]
+                    lines[k, 1, lt, 8 : 8 + rows] = w[:, cut]
+                for lt in range(lanes // 128):
+                    for t in range(rows // 16):
+
+                        def rows_of(n, off):
+                            return lines[k, n, lt, pl.ds(8 + 16 * t + off, 8, stride=2)]
+
+                        me, mo, we, wo = (
+                            rows_of(n, off) for n in range(2) for off in range(2)
+                        )
+                        next_me, next_we = rows_of(0, 2), rows_of(1, 2)
+                        m_e = mo + rows_of(0, -1)
+                        w_e = wo + rows_of(1, -1)
+                        m_o = me + next_me
+                        w_o = we + next_we
+                        m_ee = rows_of(0, -2) + next_me
+                        w_ee = rows_of(1, -2) + next_we
+                        ev = pl.ds(16 * t, 8, stride=2)
+                        od = pl.ds(16 * t + 1, 8, stride=2)
+                        acc[0, x + k, lt, ev] = 8.0 * me + 2.0 * m_e - m_ee
+                        acc[0, x + k, lt, od] = 16.0 * mo + 2.0 * m_o
+                        acc[1, x + k, lt, ev] = (22.0 * me - 6.0 * m_e) + (
+                            8.0 * we + 2.0 * w_e - w_ee
+                        )
+                        acc[1, x + k, lt, od] = (32.0 * mo - 6.0 * m_o) + (
+                            16.0 * wo + 2.0 * w_o
+                        )
+            return carry
+
+        lax.fori_loop(0, pl.cdiv(2 * pairs, 4), body, 0)
+
+    def applied(acc, first, pairs, level, use):
+        scale = 2.0**level / 2700.0
+
         def body(p, carry):
             x = first + 2 * p
-            for k in range(2):
-                a, c = y_filters(*z_filters(src[x + k]))
-                acc[0, x + k] = a
-                acc[1, x + k] = c
-            return carry
-
-        lax.fori_loop(0, pairs, body, 0)
-
-    def applied(acc, first, pairs, level, use):
-        scale = 2.0**level / 2700.0
-
-        def body(p, carry):
-            x = first + 2 * p
-            for t in range(acc.shape[2] // 8):
-                y = slice(8 * t, 8 * t + 8)
-                a = [acc[0, x + k, y] for k in range(-2, 4)]
-                c = [acc[1, x + k, y] for k in range(-2, 4)]
-                even = (14.0 * a[2] - 8.0 * (a[1] + a[3]) + (a[0] + a[4])) + (
-                    8.0 * c[2] + 2.0 * (c[1] + c[3]) - (c[0] + c[4])
-                )
-                odd = (16.0 * a[3] - 8.0 * (a[2] + a[4])) + (
-                    16.0 * c[3] + 2.0 * (c[2] + c[4])
-                )
-                use(x, 0, scale * even, t)
-                use(x + 1, 1, scale * odd, t)
+            for t in range(acc.shape[3] // 8 - 1):
+                for lt in range(acc.shape[2]):
+                    y = slice(8 * t, 8 * t + 8)
+                    a = [acc[0, x + k, lt, y] for k in range(-1, 3)]
+                    c = [acc[1, x + k, lt, y] for k in range(-2, 4)]
+                    even = (22.0 * a[1] - 6.0 * (a[0] + a[2])) + (
+                        8.0 * c[2] + 2.0 * (c[1] + c[3]) - (c[0] + c[4])
+                    )
+                    odd = (32.0 * a[2] - 6.0 * (a[1] + a[3])) + (
+                        16.0 * c[3] + 2.0 * (c[2] + c[4])
+                    )
+                    use(x, 0, scale * even, t, lt)
+                    use(x + 1, 1, scale * odd, t, lt)
             return carry
 
         lax.fori_loop(0, pairs, body, 0)
@@ -321,35 +335,35 @@
 
     gx0 = ix * bx - H
 
-    def tile(t):
-        return slice(8 * t, 8 * t + 8)
-
-    def use_residual(x, odd, av, t):
-        y = tile(t)
-        r = be[x, y] - av
-        r0[x, y] = r
-        d0[x, y] = (inv0[odd][y] * (FIRST * x_mask(0, x, gx0))) * r
-
-    filter_planes(ue, a0, 0, (bx + 16) // 2)
+    def tile(t, lt):
+        return (slice(8 * t, 8 * t + 8), slice(128 * lt, 128 * lt + 128))
+
+    def use_residual(x, odd, av, t, lt):
+        y = tile(t, lt)
+        r = be[(x, *y)] - av
+        r0[(x, *y)] = r
+        d0[(x, *y)] = (inv0[odd][y] * (FIRST * x_mask(0, x, gx0))) * r
+
+    filter_planes(ue, y0, a0, 0, (bx + 16) // 2)
     applied(a0, 2, (bx + 12) // 2, 0, use_residual)
     own0 = (slice(H, H + bx), slice(H, H + by), slice(0, bz))
     out_ref[...] = u_ref[...] + d0[own0]
 
-    def use_step(x, odd, av, t):
-        y = tile(t)
-        r = r0[x, y] - av
-        r0[x, y] = r
-        d0[x, y] = KEEP * d0[x, y] + (inv0[odd][y] * (STEP * x_mask(0, x, gx0))) * r
-
-    filter_planes(d0, a0, 2, (bx + 12) // 2)
+    def use_step(x, odd, av, t, lt):
+        y = tile(t, lt)
+        r = r0[(x, *y)] - av
+        r0[(x, *y)] = r
+        d0[(x, *y)] = KEEP * d0[(x, *y)] + (inv0[odd][y] * (STEP * x_mask(0, x, gx0))) * r
+
+    filter_planes(d0, y0, a0, 2, (bx + 12) // 2)
     applied(a0, 4, (bx + 8) // 2, 0, use_step)
     out_ref[...] += d0[own0]
 
-    def use_down(x, odd, av, t):
-        y = tile(t)
-        r0[x, y] = (r0[x, y] - av) * (mask0[y] * x_mask(0, x, gx0))
-
-    filter_planes(d0, a0, 2, (bx + 10) // 2)
+    def use_down(x, odd, av, t, lt):
+        y = tile(t, lt)
+        r0[(x, *y)] = (r0[(x, *y)] - av) * (mask0[y] * x_mask(0, x, gx0))
+
+    filter_planes(d0, y0, a0, 2, (bx + 10) // 2)
     applied(a0, 4, (bx + 6) // 2, 0, use_down)
 
     def narrowed(ref, x):
@@ -409,7 +423,9 @@
     for off in offsets[0]:
         start_if(0, off, gx_copies(off))
     g1[spot(0, 0, cx), spot(1, 0, cy)] = zin[2]
-    rows1, planes1 = cy * wy + 8, cx * wx
+    rows1, planes1 = g1.shape[1], cx * wx
+    y1[...] = jnp.zeros_like(y1)
+    y2[...] = jnp.zeros_like(y2)
     d1[...] = jnp.zeros_like(d1)
     a1[...] = jnp.zeros_like(a1)
     d2[...] = jnp.zeros_like(d2)
@@ -442,26 +458,26 @@
 
     lax.fori_loop(0, planes1 // 2, first_mid, 0)
 
-    def use_step1(x, odd, av, t):
-        y = tile(t)
-        r = r1[x, y] - av
-        r1[x, y] = r
-        d = KEEP * d1[x, y] + (inv1[odd][y] * (STEP * x_mask(1, x, gx1))) * r
-        d1[x, y] = d
-        s1[x - Q, y] += d
-
-    def use_down1(x, odd, av, t):
-        y = tile(t)
-        r1[x, y] = (r1[x, y] - av) * (mask1[y] * x_mask(1, x, gx1))
+    def use_step1(x, odd, av, t, lt):
+        y = tile(t, lt)
+        r = r1[(x, *y)] - av
+        r1[(x, *y)] = r
+        d = KEEP * d1[(x, *y)] + (inv1[odd][y] * (STEP * x_mask(1, x, gx1))) * r
+        d1[(x, *y)] = d
+        s1[(x - Q, *y)] += d
+
+    def use_down1(x, odd, av, t, lt):
+        y = tile(t, lt)
+        r1[(x, *y)] = (r1[(x, *y)] - av) * (mask1[y] * x_mask(1, x, gx1))
 
     half1 = planes1 // 2
-    filter_planes(d1, a1, Q, half1)
+    filter_planes(d1, y1, a1, Q, half1)
     applied(a1, Q, half1, 1, use_step1)
-    filter_planes(d1, a1, Q, half1)
+    filter_planes(d1, y1, a1, Q, half1)
     applied(a1, Q, half1, 1, use_down1)
 
     planes2 = planes1 // 2
-    rows2 = cy * wy // 2 + 8
+    rows2 = d2.shape[1]
     mask2, inv2 = masks_and_diagonals(
         2, rows2, wl, start_y * (cy // 2), cy * wy // 2, lambda z: z,
         lambda z: z < wl // 2, iz * (cz // 2) - ZR // 2,
@@ -479,13 +495,13 @@
         return carry
 
     lax.fori_loop(0, planes2 // 2, down_mid, 0)
-    filter_planes(d2, a2, Q, planes2 // 2)
-
-    def use_last(x, odd, av, t):
-        y = tile(t)
-        r = r2[x, y] - av
+    filter_planes(d2, y2, a2, Q, planes2 // 2)
+
+    def use_last(x, odd, av, t, lt):
+        y = tile(t, lt)
+        r = r2[(x, *y)] - av
         step = (inv2[odd][y] * (STEP * x_mask(2, x, gx2))) * r
-        d2[x, y] = (1.0 + KEEP) * d2[x, y] + step
+        d2[(x, *y)] = (1.0 + KEEP) * d2[(x, *y)] + step
 
     applied(a2, Q, planes2 // 2, 2, use_last)
 
@@ -515,24 +531,24 @@
         return carry
 
     lax.fori_loop(0, planes1 // 4, up_mid, 0)
-    filter_planes(d1, a1, Q, half1)
-
-    def use_up1(x, odd, av, t):
-        y = tile(t)
-        r = r1[x, y] - av
-        r1[x, y] = r
+    filter_planes(d1, y1, a1, Q, half1)
+
+    def use_up1(x, odd, av, t, lt):
+        y = tile(t, lt)
+        r = r1[(x, *y)] - av
+        r1[(x, *y)] = r
         d = (inv1[odd][y] * (FIRST * x_mask(1, x, gx1))) * r
-        d1[x, y] = d
-        s1[x - Q, y] += d
+        d1[(x, *y)] = d
+        s1[(x - Q, *y)] += d
 
     applied(a1, Q, half1, 1, use_up1)
-    filter_planes(d1, a1, Q, half1)
-
-    def use_final1(x, odd, av, t):
-        y = tile(t)
-        r = r1[x, y] - av
-        d = KEEP * d1[x, y] + (inv1[odd][y] * (STEP * x_mask(1, x, gx1))) * r
-        c1[x, tile(t + 1)] = s1[x - Q, y] + d
+    filter_planes(d1, y1, a1, Q, half1)
+
+    def use_final1(x, odd, av, t, lt):
+        y = tile(t, lt)
+        r = r1[(x, *y)] - av
+        d = KEEP * d1[(x, *y)] + (inv1[odd][y] * (STEP * x_mask(1, x, gx1))) * r
+        c1[(x, *tile(t + 1, lt))] = s1[(x - Q, *y)] + d
 
     applied(a1, Q, half1, 1, use_final1)
 
@@ -558,25 +574,25 @@
 
     lax.fori_loop(0, (bx + 8) // 4, up_fine, 0)
     out_ref[...] += d0[own0]
-    filter_planes(d0, a0, 4, (bx + 8) // 2)
-
-    def use_up(x, odd, av, t):
-        y = tile(t)
-        r = r0[x, y] - av
-        r0[x, y] = r
-        d0[x, y] = (inv0[odd][y] * (FIRST * x_mask(0, x, gx0))) * r
+    filter_planes(d0, y0, a0, 4, (bx + 8) // 2)
+
+    def use_up(x, odd, av, t, lt):
+        y = tile(t, lt)
+        r = r0[(x, *y)] - av
+        r0[(x, *y)] = r
+        d0[(x, *y)] = (inv0[odd][y] * (FIRST * x_mask(0, x, gx0))) * r
 
     applied(a0, 6, (bx + 4) // 2, 0, use_up)
-    filter_planes(d0, a0, 6, (bx + 4) // 2)
-
-    def use_final(x, odd, av, t):
-        if t == 0 or t == by // 8 + 1:
+    filter_planes(d0, y0, a0, 6, (bx + 4) // 2)
+
+    def use_final(x, odd, av, t, lt):
+        if t == 0 or t == by // 8 + 1 or lt >= bz // 128:
             return
-        y = tile(t)
-        r = r0[x, y] - av
-        d = d0[x, y]
+        y = tile(t, lt)
+        r = r0[(x, *y)] - av
+        d = d0[(x, *y)]
         new = d + (KEEP * d + (inv0[odd][y] * STEP) * r)
-        out_ref[x - H, tile(t - 1)] += new[:, :bz]
+        out_ref[(x - H, *tile(t - 1, lt))] += new
 
     applied(a0, H, bx // 2, 0, use_final)
 
@@ -599,8 +615,8 @@
     wy = ny if ny <= 2 * REACH + 1 else 2 * REACH + 1
     wl = cz + 2 * ZR
     rows0, lanes0 = by + 2 * H, 2 * bz
-    rows1, planes1 = cy * wy + 8, cx * wx
-    rows2, planes2 = cy * wy // 2 + 8, planes1 // 2
+    rows1, planes1 = -(-cy * wy // 16) * 16, cx * wx
+    rows2, planes2 = -(-cy * wy // 32) * 16, planes1 // 2
     crow = cy + 16
 
     def z_pos(z):
@@ -638,14 +654,15 @@
         scratch_shapes=[
             vm(bx + 16, rows0, lanes0), vm(bx + 16, rows0, lanes0),
             vm(bx + 16, rows0, lanes0), vm(bx + 16, rows0, lanes0),
-            vm(2, bx + 16, rows0, lanes0), vm(cx + 8, rows0, lanes0),
+            vm(2, bx + 16, lanes0 // 128, rows0 + 8, 128), vm(cx + 8, rows0, lanes0),
             vm(2, 2, groups, rows0, bz), vm(2, 2, groups, rows0, bz),
-            vm(cx, cy, wl), vm(3, cx, cy, wl),
+            vm(4, 2, lanes0 // 128, rows0 + 16, 128), vm(4, 2, wl // 128, rows1 + 16, 128),
+            vm(4, 2, wl // 128, rows2 + 16, 128), vm(cx, cy, wl), vm(3, cx, cy, wl),
             vm(planes1, rows1, wl), vm(planes1 + 16, rows1, wl),
             vm(planes1 + 16, rows1, wl), vm(planes1, rows1, wl),
-            vm(2, planes1 + 16, rows1, wl), vm(planes1 + 16, rows1 + 8, wl),
+            vm(2, planes1 + 16, wl // 128, rows1 + 8, 128), vm(planes1 + 16, rows1 + 16, wl),
             vm(planes2 + 16, rows2, wl), vm(planes2 + 16, rows2, wl),
-            vm(2, planes2 + 16, rows2, wl), vm(planes2 + 8, rows1, wl),
+            vm(2, planes2 + 16, wl // 128, rows2 + 8, 128), vm(planes2 + 8, rows1, wl),
             dma(16), dma(16), dma(2), dma(2),
             dma(2, 4 * REACH + 1), dma(2, 4 * REACH + 1), dma(2), dma(2),
         ],

time: 70 us -> 58.6 us (0.84)
  Pallas kernels: 68.3 us -> 56.8 us
    pallas_call x1, Pallas kernels: 68.3 us -> 56.8 us  [local(): pl.pallas_call(functools.partial(kernel, geo), out_shape=jax.ShapeDtypeSt...]
where the time goes in v3:
time: 58.6 us; the launch traced here: 58.4 us
  Pallas kernels  56.8 us (97%)
  local copies, waits for them, and re-layouts  1.57 us (3%)
    pallas_call x1, Pallas kernels, local(): pl.pallas_call(functools.partial(kernel, geo), out_shape=jax.ShapeDtypeSt...  56.8 us
    unnamed x1, local copies, waits for them, and re-layouts  1.57 us

profile of v3, /device:TPU:1, one launch (start us, length us, event | category | flops | bytes accessed | tf_op | source)
XLA Modules:
  0.0 58.4 jit_solution(11429408941095982838)
XLA Ops:
  0.0 56.8 %shard_map.100 = f32[16,16,128]{2,1,0:T(8,128)} custom-call(f32[16,16,128]{2,1,0:T(8,128)} %u_ref.1, f32[16,16,128]{2,1,0:T(8,128)} %b_ref.1, bf16[256,128]{1,0:T(8,128)(2,1)} %constant.16.clone.rz0, f32[8,32]{1,0:T(8,128)} %constant.17.clone.ry0, bf16[128,128]{1,0:T(8,128)(2,1)} %constant.18.clone.rz1, f32[16,32]{1,0:T(8,128)} %constant.19.clone.ry1, ...), custom_call_target="tpu_custom_call" | custom-call | tf_op jit(solution)/shard_map/pallas_call | solution.py:649
  56.8 1.6 %copy.12 = f32[16,16,128]{2,1,0:T(8,128)} copy(f32[16,16,128]{2,1,0:T(8,128)} %shard_map.100) | data formatting | bytes 262144
